TPU v7x, 128 devices: a whole 4x4x4 slice. The times are simulated.
128 devices in a mesh: group: 16 (over y, x_hi, core), tp: 8 (over z, x_lo).
Axes of the slice: x: 4 (x_hi: 2, x_lo: 2; x = x_hi * 2 + x_lo), y: 4, z: 4, core: 2. Of those that a mesh axis runs over, the one named last changes fastest.
Arguments:
- prefix_kv: bfloat16 [8, 16384, 256], P('tp'), may hold values from -4 to 4
- cached_node_states: bfloat16 [8, 480, 64, 256], P('tp', 'group'), may hold values from -4 to 4
- fresh_hidden: bfloat16 [2048, 8192], P(('group', 'tp')), may hold values from -6 to 6
- key_value_weight: bfloat16 [8192, 2048], P(None, 'tp'), may hold values from -0.0625 to 0.0625
- key_value_bias: bfloat16 [2048], P('tp'), may hold values from -3 to 3
- decode_q: bfloat16 [2048, 8192], P('group', 'tp'), may hold values from -128 to 128
- decoded_key_value: bfloat16 [8, 2048, 256], P('tp', 'group'), may hold values from -8 to 8
- parent: int32 [512], replicated, may hold values from -1 to 511, as said below
- child_parent: int32 [16], replicated, may hold values from 0 to 511, as said below
- node_len: int32 [512], replicated, may hold values from 1 to 64
Outputs:
- attended: bfloat16 [2048, 8192], P('group', 'tp')
Inputs may be any that keep to these rules, and one draw needn't show every extreme that they name: `parent`: node n is held by group n // 32. Parents lead from any node to a root within 64 nodes. All nodes at one depth are held by one group, and each group's nodes lie at 4 depths, 8 at each, so a path holds at most 4 nodes of one group. `child_parent`: every path from a child's parent holds at most 64 nodes and at most 4 of any group; at least one child's path has exactly 64 nodes, 4 of every group.
All inputs are finite; a program needn't handle non-finite values.
Results may differ from a plain program's by a relative error of at most 0.0038.
Values may be sent and summed in bfloat16 or wider, within the bound.
No kernel may reach another device: no remote copies, remote signals or barrier semaphores. Data moves between devices by JAX's collectives and lax.ppermute only.
A program may use at most 128 MiB of HBM per device.

v0:
```python
import jax
import jax.numpy as jnp
from jax import lax
from jax.sharding import PartitionSpec as P

STEP_SLOTS = 64
PATH_LIMIT = 64
FRESH_NODES = 2
DSTEPS = 4


very_low = -1e30


def attend(partial_value, query_matrix, key_rows, key_mask, score_scale):
    running_max, summed, numerator = partial_value
    head_size = query_matrix.shape[-1]
    scores = (
        jnp.einsum(
            "hrd,hkd->hrk",
            query_matrix,
            key_rows[..., :head_size],
            preferred_element_type=jnp.float32,
        )
        * score_scale
    )
    if key_mask is not None:
        scores = jnp.where(key_mask[None], scores, very_low)
    new_max = jnp.maximum(running_max, jnp.max(scores, axis=-1))
    weights = jnp.exp(scores - new_max[..., None])
    if key_mask is not None:
        weights = jnp.where(key_mask[None], weights, 0.0)
    factor = jnp.exp(running_max - new_max)
    summed = summed * factor + jnp.sum(weights, axis=-1)
    numerator = numerator * factor[..., None] + jnp.einsum(
        "hrk,hkd->hrd",
        weights.astype(jnp.bfloat16),
        key_rows[..., head_size:],
        preferred_element_type=jnp.float32,
    )
    return (new_max, summed, numerator)


def prefix_pass(partial_value, query_matrix, prefix_kv, score_scale):
    prefix_len = prefix_kv.shape[1]
    block_len = min(prefix_len, 2048)

    def advance(position, carried):
        key_rows = lax.dynamic_slice_in_dim(prefix_kv, position * block_len, block_len, 1)
        return attend(carried, query_matrix, key_rows, None, score_scale)

    return lax.fori_loop(0, prefix_len // block_len, advance, partial_value)


def lookup(values_table, positions):
    matches = positions[..., None] == jnp.arange(values_table.shape[0])
    return jnp.sum(jnp.where(matches, values_table, 0), axis=-1)


def all_paths(parent, child_parent, path_depth):

    def climb_up(current, unused):
        following = jnp.where(current >= 0, lookup(parent, current), -1)
        return (following, current)

    unused_end, trail_nodes = lax.scan(climb_up, child_parent, None, length=path_depth)
    return trail_nodes.T


def per_device(
    prefix_kv,
    cached_node_states,
    fresh_hidden,
    key_value_weight,
    key_value_bias,
    decode_q,
    decoded_key_value,
    parent,
    child_parent,
    node_len,
):
    kv_heads = prefix_kv.shape[0]
    head_size = prefix_kv.shape[2] // 2
    row_count = decode_q.shape[0]
    group_share = decode_q.shape[1] // (kv_heads * head_size)
    query_row_block = group_share * row_count
    group_count = lax.axis_size("group")
    my_group = lax.axis_index("group")
    per_node = parent.shape[0] // group_count
    slot_count = PATH_LIMIT // group_count
    score_scale = head_size ** (-0.5)
    query_matrix = (
        decode_q.reshape(row_count, kv_heads, group_share, head_size)
        .transpose(1, 2, 0, 3)
        .reshape(kv_heads, query_row_block, head_size)
    )
    partial_value = (
        jnp.full((kv_heads, query_row_block), very_low, jnp.float32),
        jnp.zeros((kv_heads, query_row_block), jnp.float32),
        jnp.zeros((kv_heads, query_row_block, head_size), jnp.float32),
    )
    projected = jnp.dot(
        lax.all_gather(fresh_hidden, "tp", axis=0, tiled=True),
        key_value_weight,
        preferred_element_type=jnp.float32,
    ) + key_value_bias.astype(jnp.float32)
    fresh_key_value = (
        projected.astype(jnp.bfloat16)
        .reshape(FRESH_NODES, STEP_SLOTS, kv_heads, 2 * head_size)
        .transpose(2, 0, 1, 3)
    )
    node_lookup_table = jnp.concatenate([cached_node_states, fresh_key_value], axis=1)
    trails = all_paths(parent, child_parent, PATH_LIMIT)
    my_path = lax.dynamic_index_in_dim(trails, my_group, 0, keepdims=False)
    token_index = jnp.arange(STEP_SLOTS)
    shard_kv = lax.all_gather(node_lookup_table, "group", axis=1, tiled=True)
    first_node = jnp.int32(0)
    shard_nodes = shard_kv.shape[1]
    picks = min(PATH_LIMIT, shard_nodes, slot_count * (shard_nodes // per_node + 1))
    inside = (my_path >= first_node) & (my_path < first_node + shard_nodes)
    order_rank = jnp.cumsum(inside.astype(jnp.int32)) - 1
    pick_hit = inside[:, None] & (order_rank[:, None] == jnp.arange(picks)[None, :])
    local_ids = jnp.sum(jnp.where(pick_hit, my_path[:, None], 0), axis=0)
    filled = jnp.any(pick_hit, axis=0)
    node_lens = lookup(node_len, local_ids)
    key_mask = (filled[:, None] & (token_index[None, :] < node_lens[:, None])).reshape(
        1, picks * STEP_SLOTS
    )
    key_rows = jnp.take(shard_kv, local_ids, axis=1).reshape(
        kv_heads, picks * STEP_SLOTS, 2 * head_size
    )
    partial_value = attend(partial_value, query_matrix, key_rows, key_mask, score_scale)
    partial_value = prefix_pass(partial_value, query_matrix, prefix_kv, score_scale)
    row_ids = jnp.arange(row_count)
    own_mask = (row_ids[:, None] // DSTEPS == row_ids[None, :] // DSTEPS) & (
        row_ids[None, :] % DSTEPS <= row_ids[:, None] % DSTEPS
    )
    own_mask = jnp.tile(own_mask, (group_share, 1))
    partial_value = attend(partial_value, query_matrix, decoded_key_value, own_mask, score_scale)
    running_max, summed, numerator = partial_value
    attended = numerator / summed[..., None]
    attended = attended.reshape(kv_heads, group_share, row_count, head_size).transpose(2, 0, 1, 3)
    return attended.reshape(row_count, kv_heads * group_share * head_size).astype(jnp.bfloat16)


def solution(mesh):
    placed = (
        P("tp", None, None),
        P("tp", "group", None, None),
        P(("group", "tp"), None),
        P(None, "tp"),
        P("tp"),
        P("group", "tp"),
        P("tp", "group", None),
        P(),
        P(),
        P(),
    )
    return jax.shard_map(
        per_device, mesh=mesh, in_specs=placed, out_specs=P("group", "tp"), check_vma=False
    )
```

profile of v0, /device:TPU:1, one launch (start us, length us, event | category | flops | bytes accessed | tf_op | source)
XLA Modules:
  0.0 307.1 jit_solution(17969215304217784282)
XLA Ops:
  8.0 55.8 %all-gather.3.cloned.1.call-done = bf16[128,8192]{1,0:T(8,128)(2,1)} async-done(((bf16[16,8192]{1,0:T(8,128)(2,1)}), bf16[128,8192]{1,0:T(8,128)(2,1)}) %all-gather.3.cloned.1.call-update) | async-done | bytes 2097168 | tf_op jit(solution)/shard_map/all_gather | solution.py:103
  63.8 3.5 %fusion.31 = bf16[128,256]{1,0:T(8,128)(2,1)S(1)} fusion(bf16[128,8192]{1,0:T(8,128)(2,1)} %all-gather.3.cloned.1.call-done, bf16[8192,256]{1,0:T(8,128)(2,1)} %param.17, f32[256]{0:T(256)S(1)} %convert_element_type.40), kind=kOutput, calls=%fused_computation.37 | convolution fusion | flops 536936448 | bytes 6358016 | tf_op jit(solution)/shard_map/dot_general | solution.py:102
  69.7 15.6 %while.29 = (s32[]{:T(128)}, s32[16]{0:T(128)S(1)}, s32[64,16]{1,0:T(8,128)S(1)}, s32[512]{0:T(512)S(1)}, s32[]{:T(128)}, /*index=5*/s32[]{:T(128)}) while((s32[]{:T(128)}, s32[16]{0:T(128)S(1)}, s32[64,16]{1,0:T(8,128)S(1)}, s32[512]{0:T(512)S(1)}, s32[]{:T(128)}, /*index=5*/s32[]{:T(128)}) %tuple.66), condition=%wide.region_2.3_spmd, body=%wide.region_0.2_spmd.sunk | while | flops 24594 | bytes 2569 | solution.py:66
  87.1 91.8 %all-gather.5.cloned.1.call-done = bf16[1,512,64,256]{3,2,0,1:T(8,128)(2,1)} async-done(((bf16[1,32,64,256]{3,2,0,1:T(8,128)(2,1)}), bf16[1,512,64,256]{3,2,0,1:T(8,128)(2,1)}) %all-gather.5.cloned.1.call-update) | async-done | bytes 16777232 | tf_op jit(solution)/shard_map/all_gather | solution.py:116
  178.8 6.4 %gather_fusion = bf16[64,64,256]{2,1,0:T(8,128)(2,1)S(1)} fusion(bf16[512,64,256]{2,1,0:T(8,128)(2,1)} %bitcast.139, s32[1024]{0:T(1024)S(1)} %pad_clamp_fusion), kind=kCustom, calls=%fused_computation | custom fusion | bytes 4194560 | tf_op jit(solution)/shard_map/jit(_take)/gather | solution.py:129
  187.4 4.1 %fusion.15 = (f32[1024]{0:T(1024)S(1)}, f32[4096,1024]{1,0:T(8,128)S(1)}) fusion(pred[4096]{0:T(1024)(128)(4,1)S(1)} %and.109, bf16[1024,128]{1,0:T(8,128)(2,1)S(1)} %bitcast.122, bf16[1,4096,256]{2,1,0:T(8,128)(2,1)S(1)} %bitcast_select_fusion), kind=kOutput, calls=%fused_computation.22 | convolution fusion | flops 1086323712 | bytes 18096128 | tf_op jit(solution)/shard_map/hrd,hkd->hrk/dot_general | solution.py:19
  191.6 4.2 %fusion.16 = f32[1024]{0:T(1024)S(1)} fusion(f32[4096,1024]{1,0:T(8,128)S(1)} %get-tuple-element.173, f32[1024]{0:T(1024)S(1)} %get-tuple-element.171, pred[4096]{0:T(1024)(128)(4,1)S(1)} %and.109), kind=kLoop, calls=%fused_computation.23 | loop fusion | flops 20970496 | bytes 16789504 | tf_op jit(solution)/shard_map/reduce_sum | solution.py:34
  195.8 5.7 %fusion.27 = f32[1,1024,128]{2,1,0:T(8,128)S(1)} fusion(f32[4096,1024]{1,0:T(8,128)S(1)} %get-tuple-element.173, f32[1024]{0:T(1024)S(1)} %get-tuple-element.171, pred[4096]{0:T(1024)(128)(4,1)S(1)} %and.109, bf16[1,4096,256]{2,1,0:T(8,128)(2,1)S(1)} %bitcast_select_fusion, f32[1024]{0:T(1024)S(1)} %get-tuple-element.170), kind=kOutput, calls=%fused_computation.34 | convolution fusion | flops 1094844416 | bytes 18362368 | tf_op jit(solution)/shard_map/hrk,hkd->hrd/dot_general | solution.py:35
  201.5 97.1 %while.30 = (s32[]{:T(128)}, f32[1,1024]{1,0:T(1,128)S(1)}, f32[1,1024]{1,0:T(1,128)S(1)}, f32[1,1024,128]{2,1,0:T(8,128)S(1)}, bf16[1,16384,256]{2,1,0:T(8,128)...) while((s32[]{:T(128)}, f32[1,1024]{1,0:T(1,128)S(1)}, ...), condition=%wide.region_12.13_spmd, body=%wide.region_9.12_spmd.sunk | while | flops 1090783232 | bytes 61145292 | solution.py:52
  204.0 3.2 %copy-done = f32[2048,1024]{1,0:T(8,128)} copy-done((f32[2048,1024]{1,0:T(8,128)}, f32[2048,1024]{1,0:T(8,128)S(1)}, u32[]{:S(2)}) %copy-start) | copy-done | bytes 8388632 | tf_op jit(solution)/shard_map/while
  208.7 5.1 %fusion.62 = f32[1,1024,128]{2,1,0:T(8,128)S(1)} fusion(f32[2048,1024]{1,0:T(8,128)} %copy-done, f32[1024]{0:T(1024)S(1)} %bitcast.126, bf16[1,16384,256]{2,1,0:T(8,128)(2,1)} %get-tuple-element.292, s32[]{:T(128)S(6)} %select_n.180, s32[]{:T(128)S(6)} %add.179, f32[1,1024,128]{2,1,0:T(8,128)S(1)} %get-tuple-element.280, f32[1024]{0:T(1024)S(1)} %bitcast.127), kind=kOutput, calls=%fused_computation.10.clone.1 | convolution fusion | flops 543424512 | bytes 9969672 | tf_op jit(solution)/shard_map/while/body/eval_jaxpr/hrk,hkd->hrd/dot_general | solution.py:35
  213.8 2.3 multiply_reduce_fusion.2
  216.2 3.2 %copy-done = f32[2048,1024]{1,0:T(8,128)} copy-done((f32[2048,1024]{1,0:T(8,128)}, f32[2048,1024]{1,0:T(8,128)S(1)}, u32[]{:S(2)}) %copy-start) | copy-done | bytes 8388632 | tf_op jit(solution)/shard_map/while
  220.8 5.1 %fusion.62 = f32[1,1024,128]{2,1,0:T(8,128)S(1)} fusion(f32[2048,1024]{1,0:T(8,128)} %copy-done, f32[1024]{0:T(1024)S(1)} %bitcast.126, bf16[1,16384,256]{2,1,0:T(8,128)(2,1)} %get-tuple-element.292, s32[]{:T(128)S(6)} %select_n.180, s32[]{:T(128)S(6)} %add.179, f32[1,1024,128]{2,1,0:T(8,128)S(1)} %get-tuple-element.280, f32[1024]{0:T(1024)S(1)} %bitcast.127), kind=kOutput, calls=%fused_computation.10.clone.1 | convolution fusion | flops 543424512 | bytes 9969672 | tf_op jit(solution)/shard_map/while/body/eval_jaxpr/hrk,hkd->hrd/dot_general | solution.py:35
  225.9 2.3 multiply_reduce_fusion.2
  228.3 3.2 %copy-done = f32[2048,1024]{1,0:T(8,128)} copy-done((f32[2048,1024]{1,0:T(8,128)}, f32[2048,1024]{1,0:T(8,128)S(1)}, u32[]{:S(2)}) %copy-start) | copy-done | bytes 8388632 | tf_op jit(solution)/shard_map/while
  232.9 5.1 %fusion.62 = f32[1,1024,128]{2,1,0:T(8,128)S(1)} fusion(f32[2048,1024]{1,0:T(8,128)} %copy-done, f32[1024]{0:T(1024)S(1)} %bitcast.126, bf16[1,16384,256]{2,1,0:T(8,128)(2,1)} %get-tuple-element.292, s32[]{:T(128)S(6)} %select_n.180, s32[]{:T(128)S(6)} %add.179, f32[1,1024,128]{2,1,0:T(8,128)S(1)} %get-tuple-element.280, f32[1024]{0:T(1024)S(1)} %bitcast.127), kind=kOutput, calls=%fused_computation.10.clone.1 | convolution fusion | flops 543424512 | bytes 9969672 | tf_op jit(solution)/shard_map/while/body/eval_jaxpr/hrk,hkd->hrd/dot_general | solution.py:35
  238.1 2.3 multiply_reduce_fusion.2
  240.4 3.2 %copy-done = f32[2048,1024]{1,0:T(8,128)} copy-done((f32[2048,1024]{1,0:T(8,128)}, f32[2048,1024]{1,0:T(8,128)S(1)}, u32[]{:S(2)}) %copy-start) | copy-done | bytes 8388632 | tf_op jit(solution)/shard_map/while
  245.0 5.1 %fusion.62 = f32[1,1024,128]{2,1,0:T(8,128)S(1)} fusion(f32[2048,1024]{1,0:T(8,128)} %copy-done, f32[1024]{0:T(1024)S(1)} %bitcast.126, bf16[1,16384,256]{2,1,0:T(8,128)(2,1)} %get-tuple-element.292, s32[]{:T(128)S(6)} %select_n.180, s32[]{:T(128)S(6)} %add.179, f32[1,1024,128]{2,1,0:T(8,128)S(1)} %get-tuple-element.280, f32[1024]{0:T(1024)S(1)} %bitcast.127), kind=kOutput, calls=%fused_computation.10.clone.1 | convolution fusion | flops 543424512 | bytes 9969672 | tf_op jit(solution)/shard_map/while/body/eval_jaxpr/hrk,hkd->hrd/dot_general | solution.py:35
  250.2 2.3 multiply_reduce_fusion.2
  252.5 3.2 %copy-done = f32[2048,1024]{1,0:T(8,128)} copy-done((f32[2048,1024]{1,0:T(8,128)}, f32[2048,1024]{1,0:T(8,128)S(1)}, u32[]{:S(2)}) %copy-start) | copy-done | bytes 8388632 | tf_op jit(solution)/shard_map/while
  257.2 5.1 %fusion.62 = f32[1,1024,128]{2,1,0:T(8,128)S(1)} fusion(f32[2048,1024]{1,0:T(8,128)} %copy-done, f32[1024]{0:T(1024)S(1)} %bitcast.126, bf16[1,16384,256]{2,1,0:T(8,128)(2,1)} %get-tuple-element.292, s32[]{:T(128)S(6)} %select_n.180, s32[]{:T(128)S(6)} %add.179, f32[1,1024,128]{2,1,0:T(8,128)S(1)} %get-tuple-element.280, f32[1024]{0:T(1024)S(1)} %bitcast.127), kind=kOutput, calls=%fused_computation.10.clone.1 | convolution fusion | flops 543424512 | bytes 9969672 | tf_op jit(solution)/shard_map/while/body/eval_jaxpr/hrk,hkd->hrd/dot_general | solution.py:35
  262.3 2.3 multiply_reduce_fusion.2
  264.6 3.2 %copy-done = f32[2048,1024]{1,0:T(8,128)} copy-done((f32[2048,1024]{1,0:T(8,128)}, f32[2048,1024]{1,0:T(8,128)S(1)}, u32[]{:S(2)}) %copy-start) | copy-done | bytes 8388632 | tf_op jit(solution)/shard_map/while
  269.3 5.1 %fusion.62 = f32[1,1024,128]{2,1,0:T(8,128)S(1)} fusion(f32[2048,1024]{1,0:T(8,128)} %copy-done, f32[1024]{0:T(1024)S(1)} %bitcast.126, bf16[1,16384,256]{2,1,0:T(8,128)(2,1)} %get-tuple-element.292, s32[]{:T(128)S(6)} %select_n.180, s32[]{:T(128)S(6)} %add.179, f32[1,1024,128]{2,1,0:T(8,128)S(1)} %get-tuple-element.280, f32[1024]{0:T(1024)S(1)} %bitcast.127), kind=kOutput, calls=%fused_computation.10.clone.1 | convolution fusion | flops 543424512 | bytes 9969672 | tf_op jit(solution)/shard_map/while/body/eval_jaxpr/hrk,hkd->hrd/dot_general | solution.py:35
  274.4 2.3 multiply_reduce_fusion.2
  276.7 3.2 %copy-done = f32[2048,1024]{1,0:T(8,128)} copy-done((f32[2048,1024]{1,0:T(8,128)}, f32[2048,1024]{1,0:T(8,128)S(1)}, u32[]{:S(2)}) %copy-start) | copy-done | bytes 8388632 | tf_op jit(solution)/shard_map/while
  281.4 5.1 %fusion.62 = f32[1,1024,128]{2,1,0:T(8,128)S(1)} fusion(f32[2048,1024]{1,0:T(8,128)} %copy-done, f32[1024]{0:T(1024)S(1)} %bitcast.126, bf16[1,16384,256]{2,1,0:T(8,128)(2,1)} %get-tuple-element.292, s32[]{:T(128)S(6)} %select_n.180, s32[]{:T(128)S(6)} %add.179, f32[1,1024,128]{2,1,0:T(8,128)S(1)} %get-tuple-element.280, f32[1024]{0:T(1024)S(1)} %bitcast.127), kind=kOutput, calls=%fused_computation.10.clone.1 | convolution fusion | flops 543424512 | bytes 9969672 | tf_op jit(solution)/shard_map/while/body/eval_jaxpr/hrk,hkd->hrd/dot_general | solution.py:35
  286.5 2.3 multiply_reduce_fusion.2
  288.9 3.2 %copy-done = f32[2048,1024]{1,0:T(8,128)} copy-done((f32[2048,1024]{1,0:T(8,128)}, f32[2048,1024]{1,0:T(8,128)S(1)}, u32[]{:S(2)}) %copy-start) | copy-done | bytes 8388632 | tf_op jit(solution)/shard_map/while
  293.5 5.1 %fusion.62 = f32[1,1024,128]{2,1,0:T(8,128)S(1)} fusion(f32[2048,1024]{1,0:T(8,128)} %copy-done, f32[1024]{0:T(1024)S(1)} %bitcast.126, bf16[1,16384,256]{2,1,0:T(8,128)(2,1)} %get-tuple-element.292, s32[]{:T(128)S(6)} %select_n.180, s32[]{:T(128)S(6)} %add.179, f32[1,1024,128]{2,1,0:T(8,128)S(1)} %get-tuple-element.280, f32[1024]{0:T(1024)S(1)} %bitcast.127), kind=kOutput, calls=%fused_computation.10.clone.1 | convolution fusion | flops 543424512 | bytes 9969672 | tf_op jit(solution)/shard_map/while/body/eval_jaxpr/hrk,hkd->hrd/dot_general | solution.py:35
  (281 shorter events, 38.0 us)
Async XLA Ops:
  6.5 79.9 %copy-start.1 = (bf16[128,1024]{1,0:T(8,128)(2,1)S(1)}, bf16[128,1024]{1,0:T(8,128)(2,1)}, u32[]{:S(2)}) copy-start(bf16[128,1024]{1,0:T(8,128)(2,1)} %param.19) | copy-start | bytes 786436
  6.5 80.3 %copy-start.5 = (bf16[1,128,256]{2,1,0:T(8,128)(2,1)S(1)}, bf16[1,128,256]{2,1,0:T(8,128)(2,1)}, u32[]{:S(2)}) copy-start(bf16[1,128,256]{2,1,0:T(8,128)(2,1)} %param.20) | copy-start | bytes 196612
  6.5 63.1 %copy-start.2 = (s32[512]{0:T(512)S(1)}, s32[512]{0:T(512)}, u32[]{:S(2)}) copy-start(s32[512]{0:T(512)} %param.21) | copy-start | bytes 6148
  6.5 63.1 %copy-start.3 = (s32[16]{0:T(128)S(1)}, s32[16]{0:T(128)}, u32[]{:S(2)}) copy-start(s32[16]{0:T(128)} %param.22) | copy-start | bytes 196
  6.5 79.6 %copy-start.4 = (s32[512]{0:T(512)S(1)}, s32[512]{0:T(512)}, u32[]{:S(2)}) copy-start(s32[512]{0:T(512)} %param.23) | copy-start | bytes 6148
  6.5 57.3 %all-gather.3.cloned.1.call-start = ((), (), s32[]{:S(2)}) async-start(), calls=%async_computation | async-start | bytes 2359296 | tf_op jit(solution)/shard_map/all_gather | solution.py:103
  7.3 171.6 %all-gather.5.cloned.1.call-start = ((), (), s32[]{:S(2)}) async-start(), calls=%async_computation.1 | async-start | bytes 17825792 | tf_op jit(solution)/shard_map/all_gather | solution.py:116
  204.0 3.2 %copy-start = (f32[2048,1024]{1,0:T(8,128)}, f32[2048,1024]{1,0:T(8,128)S(1)}, u32[]{:S(2)}) copy-start(f32[2048,1024]{1,0:T(8,128)S(1)} %get-tuple-element.245) | copy-start | bytes 25165828 | tf_op jit(solution)/shard_map/while
  216.1 3.2 %copy-start = (f32[2048,1024]{1,0:T(8,128)}, f32[2048,1024]{1,0:T(8,128)S(1)}, u32[]{:S(2)}) copy-start(f32[2048,1024]{1,0:T(8,128)S(1)} %get-tuple-element.245) | copy-start | bytes 25165828 | tf_op jit(solution)/shard_map/while
  228.2 3.2 %copy-start = (f32[2048,1024]{1,0:T(8,128)}, f32[2048,1024]{1,0:T(8,128)S(1)}, u32[]{:S(2)}) copy-start(f32[2048,1024]{1,0:T(8,128)S(1)} %get-tuple-element.245) | copy-start | bytes 25165828 | tf_op jit(solution)/shard_map/while
  240.4 3.2 %copy-start = (f32[2048,1024]{1,0:T(8,128)}, f32[2048,1024]{1,0:T(8,128)S(1)}, u32[]{:S(2)}) copy-start(f32[2048,1024]{1,0:T(8,128)S(1)} %get-tuple-element.245) | copy-start | bytes 25165828 | tf_op jit(solution)/shard_map/while
  252.5 3.2 %copy-start = (f32[2048,1024]{1,0:T(8,128)}, f32[2048,1024]{1,0:T(8,128)S(1)}, u32[]{:S(2)}) copy-start(f32[2048,1024]{1,0:T(8,128)S(1)} %get-tuple-element.245) | copy-start | bytes 25165828 | tf_op jit(solution)/shard_map/while
  264.6 3.2 %copy-start = (f32[2048,1024]{1,0:T(8,128)}, f32[2048,1024]{1,0:T(8,128)S(1)}, u32[]{:S(2)}) copy-start(f32[2048,1024]{1,0:T(8,128)S(1)} %get-tuple-element.245) | copy-start | bytes 25165828 | tf_op jit(solution)/shard_map/while
  276.7 3.2 %copy-start = (f32[2048,1024]{1,0:T(8,128)}, f32[2048,1024]{1,0:T(8,128)S(1)}, u32[]{:S(2)}) copy-start(f32[2048,1024]{1,0:T(8,128)S(1)} %get-tuple-element.245) | copy-start | bytes 25165828 | tf_op jit(solution)/shard_map/while
  288.8 3.2 %copy-start = (f32[2048,1024]{1,0:T(8,128)}, f32[2048,1024]{1,0:T(8,128)S(1)}, u32[]{:S(2)}) copy-start(f32[2048,1024]{1,0:T(8,128)S(1)} %get-tuple-element.245) | copy-start | bytes 25165828 | tf_op jit(solution)/shard_map/while
Sparse Core Ops, SparseCore 0:
  9.0 54.7 all-gather.2
  69.8 109.0 all-gather.4
where the time goes:
time: 308 us; the launch traced here: 307 us
  waiting for transfers between devices  148 us (48%)
  matrix products  73.2 us (24%)
  local copies, waits for them, and re-layouts  36 us (12%)
  other arithmetic  34.5 us (11%)
  between operations  13.7 us (4%)
    all_gather x1, waiting for transfers between devices, per_device(): shard_kv = lax.all_gather(node_lookup_table, 'group', axis=1, tiled=True)  91.8 us
    all_gather x1, waiting for transfers between devices, per_device(): lax.all_gather(fresh_hidden, 'tp', axis=0, tiled=True)  55.8 us
    dot_general x10, matrix products, attend(): jnp.einsum('hrk,hkd->hrd', weights.astype(jnp.bfloat16), key_rows[..., he...  46.9 us
    while x24, local copies, waits for them, and re-layouts  25.6 us
    dot_general x10, matrix products, attend(): jnp.einsum('hrd,hkd->hrk', query_matrix, key_rows[..., :head_size], prefe...  22.8 us
    reduce_sum x10, other arithmetic, attend(): summed = summed * factor + jnp.sum(weights, axis=-1)  15.8 us
    reduce_sum x65, other arithmetic, lookup(): return jnp.sum(jnp.where(matches, values_table, 0), axis=-1)  11.9 us
    gather x1, local copies, waits for them, and re-layouts, per_device(): jnp.take(shard_kv, local_ids, axis=1)  6.45 us
  transfers between devices with their start and end apart: 2, of which 2 were waited for; matrix products, arithmetic and copies ran while one was open for 6% of the time, Pallas kernels for 0%

commit v1 on v0

v1 whole, which is shorter than its diff:
```python
import functools

import jax
import jax.numpy as jnp
from jax import lax
from jax.experimental import pallas as pl
from jax.experimental.pallas import tpu as pltpu
from jax.sharding import PartitionSpec as P

SLOTS = 4
FRESH = 2
SUB = 512
ROWS = 256
BLOCK = 4096
FIRST_BLOCKS = 2
LOW = -1e30
LOG2E = 1.4426950408889634
VMEM_LIMIT = 48 * 2**20


def spec(shape):
    return pl.BlockSpec(shape, lambda *_: (0,) * len(shape))


def lookup(parts, positions):
    low, high = positions & 127, positions >> 7
    result = jnp.zeros_like(positions)
    for row, part in enumerate(parts):
        table = jnp.broadcast_to(part, positions.shape)
        result = jnp.where(high == row, jnp.take_along_axis(table, low, axis=1), result)
    return result


def rows_of(table):
    return [table[row : row + 1, :] for row in range(table.shape[0])]


def ranks(flags):
    width = flags.shape[1]
    before = lax.broadcasted_iota(jnp.int32, (width, width), 0) < lax.broadcasted_iota(
        jnp.int32, (width, width), 1
    )
    return jnp.dot(
        flags.astype(jnp.bfloat16), before.astype(jnp.bfloat16), preferred_element_type=jnp.float32
    )


def slot_sums(held, values, inner, cached_nodes):
    cached = held & (inner < cached_nodes)
    fresh = held & (inner >= cached_nodes)
    rank_cached = ranks(jnp.where(cached, 1.0, 0.0))
    rank_fresh = (SLOTS - 1) - ranks(jnp.where(fresh, 1.0, 0.0))
    slot = jnp.where(cached, rank_cached, rank_fresh)
    return [
        jnp.sum(jnp.where(held & (slot == float(s)), values, 0.0), axis=1, keepdims=True)
        for s in range(SLOTS)
    ]


def route_kernel(groups, parent_ref, child_ref, len_ref, cached_ref, pick_ref, bias_a_ref, bias_b_ref, send_ref, pick_v, pick_s, sem):
    me = lax.axis_index("group")
    cached_nodes = cached_ref.shape[0]
    per_node = cached_nodes + FRESH
    width = 128
    parent = parent_ref[...]
    none = parent.shape[0] * 128
    jump = jnp.where(parent < 0, none, parent)
    lane = lax.broadcasted_iota(jnp.int32, (groups, width), 1)
    path = jnp.where(lane == 0, child_ref[...], none)
    reach = 1
    while reach < 64:
        tables = rows_of(jump)
        ahead = jnp.where(path < none, lookup(tables, jnp.minimum(path, none - 1)), none)
        path = jnp.where((lane >= reach) & (lane < 2 * reach), pltpu.roll(ahead, reach, 1), path)
        jump = jnp.where(jump < none, lookup(tables, jnp.minimum(jump, none - 1)), none)
        reach *= 2
    inner = path % per_node
    there = path < none
    picks = slot_sums(
        there & (path // per_node == me), inner.astype(jnp.float32), inner, cached_nodes
    )
    pick = jnp.zeros((groups, width), jnp.float32)
    for s in range(SLOTS):
        pick = jnp.where(lane == s, picks[s], pick)
    pick = pick.astype(jnp.int32)
    pick_v[...] = pick
    pick_ref[...] = pick
    copy = pltpu.make_async_copy(pick_v, pick_s, sem)
    copy.start()
    group_row = lax.broadcasted_iota(jnp.int32, (groups, width), 0)
    mine = jnp.sum(jnp.where(group_row == me, path, 0).astype(jnp.float32), axis=0, keepdims=True)
    mine = jnp.broadcast_to(mine, (groups, width)).astype(jnp.int32)
    there = mine < none
    lengths = lookup(rows_of(len_ref[...]), jnp.minimum(mine, none - 1)).astype(jnp.float32)
    valid = slot_sums(
        there & (mine // per_node == group_row), lengths, mine % per_node, cached_nodes
    )
    half = width // 2
    token = (lane % half).astype(jnp.float32)
    for ref, first in ((bias_a_ref, 0), (bias_b_ref, 2)):
        limit = jnp.where(lane < half, valid[first], valid[first + 1])
        ref[...] = jnp.where(token < limit, 0.0, LOW)
    copy.wait()
    for g in range(groups):
        for s in range(2):
            node = jnp.minimum(pick_s[g, s], cached_nodes - 1)
            send_ref[g, s] = cached_ref[node]


def route(parent, child_parent, node_len, cached):
    groups = child_parent.shape[0]
    nodes, tokens, width = cached.shape
    rows = parent.shape[0] // 128
    table = jax.ShapeDtypeStruct((groups, 128), jnp.int32)
    bias = jax.ShapeDtypeStruct((groups, 128), jnp.float32)
    out = (table, bias, bias, jax.ShapeDtypeStruct((groups, 2, tokens, width), cached.dtype))
    args = (
        parent.reshape(rows, 128),
        jnp.broadcast_to(child_parent[:, None], (groups, 128)),
        node_len.reshape(rows, 128),
        cached,
    )
    return pl.pallas_call(
        functools.partial(route_kernel, groups),
        out_shape=out,
        in_specs=[spec(a.shape) for a in args],
        out_specs=[spec(o.shape) for o in out],
        scratch_shapes=[
            pltpu.VMEM((groups, 128), jnp.int32),
            pltpu.SMEM((groups, 128), jnp.int32),
            pltpu.SemaphoreType.DMA,
        ],
        name="route",
    )(*args)


def fresh_kernel(pick_ref, hidden_ref, weight_ref, bias_ref, cached_ref, send_ref, total, table):
    step = pl.program_id(0)
    cached_nodes, tokens, width = cached_ref.shape

    @pl.when(step == 0)
    def _():
        total[...] = jnp.zeros_like(total)
        table[:cached_nodes] = cached_ref[...]

    total[...] += jnp.dot(hidden_ref[...], weight_ref[...], preferred_element_type=jnp.float32)

    @pl.when(step == pl.num_programs(0) - 1)
    def _():
        rows = (total[...] + bias_ref[...].astype(jnp.float32)).astype(jnp.bfloat16)
        for f in range(FRESH):
            table[cached_nodes + f] = rows[f * tokens : (f + 1) * tokens]
        for g in range(send_ref.shape[0]):
            for s in range(2):
                node = jnp.clip(pick_ref[g, 2 + s], 0, cached_nodes + FRESH - 1)
                send_ref[g, s] = table[node]


def project_fresh(pick, hidden, weight, bias, cached):
    groups = pick.shape[0]
    nodes, tokens, width = cached.shape
    rows, depth = hidden.shape
    step = 2048
    return pl.pallas_call(
        fresh_kernel,
        grid=(depth // step,),
        out_shape=jax.ShapeDtypeStruct((groups, 2, tokens, width), cached.dtype),
        in_specs=[
            pl.BlockSpec(memory_space=pltpu.SMEM),
            pl.BlockSpec((rows, step), lambda i: (0, i)),
            pl.BlockSpec((step, width), lambda i: (i, 0)),
            spec((1, width)),
            spec(cached.shape),
        ],
        out_specs=spec((groups, 2, tokens, width)),
        scratch_shapes=[
            pltpu.VMEM((rows, width), jnp.float32),
            pltpu.VMEM((nodes + FRESH, tokens, width), cached.dtype),
        ],
        cost_estimate=pl.CostEstimate(
            flops=2 * rows * depth * width, bytes_accessed=8 * 2**20, transcendentals=0
        ),
        name="fresh",
    )(pick, hidden, weight, bias.reshape(1, width), cached)


def take_keys(query, maximum, total, pieces, scale):
    rows = query.shape[0]
    head = query.shape[1]

    def score(c, piece):
        kv, adjust = piece
        s = lax.dot_general(
            query[c * ROWS : (c + 1) * ROWS, :],
            kv[:, :head],
            (((1,), (1,)), ((), ())),
            preferred_element_type=jnp.float32,
        )
        return s if adjust is None else adjust(s)

    def peak(s):
        top = s[:, :128]
        for k in range(1, s.shape[1] // 128):
            top = jnp.maximum(top, s[:, k * 128 : (k + 1) * 128])
        return top

    chunks = rows // ROWS
    now = [score(0, piece) for piece in pieces]
    for c in range(chunks):
        at = slice(c * ROWS, (c + 1) * ROWS)
        top = peak(now[0])
        for s in now[1:]:
            top = jnp.maximum(top, peak(s))
        old = maximum[at, :]
        new = jnp.maximum(old, jnp.max(top, axis=1, keepdims=True) * scale)
        maximum[at, :] = new
        factor = jnp.exp2(old - new)
        acc = total[at, :] * jnp.concatenate([factor, factor], axis=1)
        later = []
        for piece, s in zip(pieces, now):
            if c + 1 < chunks:
                later.append(score(c + 1, piece))
            weights = jnp.exp2(s * scale - new[:, :1]).astype(jnp.bfloat16)
            kv = piece[0]
            values = jnp.concatenate(
                [kv[:, head:], jnp.ones((kv.shape[0], head), jnp.bfloat16)], axis=1
            )
            acc = acc + jnp.dot(weights, values, preferred_element_type=jnp.float32)
        total[at, :] = acc
        now = later


def plain_pieces(ref):
    return [(ref.at[pl.ds(k, SUB), :], None) for k in range(0, ref.shape[0], SUB)]


def masked_pieces(ref, bias_ref):
    def adjust(k, s):
        bias = [bias_ref[row : row + 1, :] for row in range(k // 128, (k + SUB) // 128)]
        return s + jnp.concatenate(bias, axis=1)

    return [
        (ref.at[pl.ds(k, SUB), :], functools.partial(adjust, k))
        for k in range(0, ref.shape[0], SUB)
    ]


def own_piece(ref, steps):
    count = ref.shape[0]

    def adjust(s):
        row = lax.broadcasted_iota(jnp.int32, s.shape, 0) % count
        key = lax.broadcasted_iota(jnp.int32, s.shape, 1)
        seen = (row // steps == key // steps) & (key <= row)
        return jnp.where(seen, s, LOW)

    return [(ref.at[pl.ds(0, count), :], adjust)]


def load_query(q_ref, query):
    rows, head = q_ref.shape[0], query.shape[1]
    for j in range(q_ref.shape[1] // head):
        query[j * rows : (j + 1) * rows, :] = q_ref[:, j * head : (j + 1) * head]


def first_kernel(scale, q_ref, prefix_ref, max_ref, total_ref, query):
    @pl.when(pl.program_id(0) == 0)
    def _():
        load_query(q_ref, query)
        max_ref[...] = jnp.full_like(max_ref, LOW)
        total_ref[...] = jnp.zeros_like(total_ref)

    take_keys(query, max_ref, total_ref, plain_pieces(prefix_ref), scale)


def middle_kernel(scale, steps, blocks, q_ref, prefix_ref, path_ref, bias_ref, own_ref, max_in, total_in, max_ref, total_ref, query):
    step = pl.program_id(0)

    @pl.when(step == 0)
    def _():
        load_query(q_ref, query)
        max_ref[...] = max_in[...]
        total_ref[...] = total_in[...]

    @pl.when(step < blocks)
    def _():
        take_keys(query, max_ref, total_ref, plain_pieces(prefix_ref), scale)

    @pl.when(step == blocks)
    def _():
        pieces = masked_pieces(path_ref, bias_ref) + own_piece(own_ref, steps)
        take_keys(query, max_ref, total_ref, pieces, scale)


def last_kernel(scale, q_ref, path_ref, bias_ref, max_in, total_in, out_ref, query, maximum, total):
    load_query(q_ref, query)
    maximum[...] = max_in[...]
    total[...] = total_in[...]
    take_keys(query, maximum, total, masked_pieces(path_ref, bias_ref), scale)
    rows, head = q_ref.shape[0], query.shape[1]
    for j in range(q_ref.shape[1] // head):
        at = slice(j * rows, (j + 1) * rows)
        out_ref[:, j * head : (j + 1) * head] = (total[at, :head] / total[at, head:]).astype(
            out_ref.dtype
        )


def attention_cost(rows, head, keys):
    return pl.CostEstimate(
        flops=8 * rows * head * keys,
        bytes_accessed=4 * keys * head,
        transcendentals=rows * keys,
    )


def per_device(
    prefix_kv,
    cached_node_states,
    fresh_hidden,
    key_value_weight,
    key_value_bias,
    decode_q,
    decoded_key_value,
    parent,
    child_parent,
    node_len,
):
    steps = 4
    head = prefix_kv.shape[2] // 2
    scale = head ** (-0.5) * LOG2E
    prefix, cached, own = prefix_kv[0], cached_node_states[0], decoded_key_value[0]
    rows = decode_q.shape[0]
    queries = rows * (decode_q.shape[1] // head)
    tp = lax.axis_size("tp")

    hidden = lax.all_to_all(
        jnp.broadcast_to(fresh_hidden[None], (tp,) + fresh_hidden.shape), "tp", 0, 0, tiled=True
    ).reshape(tp * fresh_hidden.shape[0], fresh_hidden.shape[1])
    pick, bias_a, bias_b, send_a = route(parent, child_parent, node_len, cached)
    path_a = lax.all_to_all(send_a, "group", 0, 0, tiled=True).reshape(-1, 2 * head)

    state = (
        jax.ShapeDtypeStruct((queries, 128), jnp.float32),
        jax.ShapeDtypeStruct((queries, 2 * head), jnp.float32),
    )
    params = pltpu.CompilerParams(vmem_limit_bytes=VMEM_LIMIT)
    query_scratch = pltpu.VMEM((queries, head), jnp.bfloat16)
    all_blocks = prefix.shape[0] // BLOCK
    blocks = all_blocks - FIRST_BLOCKS
    maximum, total = pl.pallas_call(
        functools.partial(first_kernel, scale),
        grid=(FIRST_BLOCKS,),
        out_shape=state,
        in_specs=[spec(decode_q.shape), pl.BlockSpec((BLOCK, 2 * head), lambda i: (i, 0))],
        out_specs=[spec(s.shape) for s in state],
        scratch_shapes=[query_scratch],
        compiler_params=params,
        cost_estimate=attention_cost(queries, head, FIRST_BLOCKS * BLOCK),
        name="attend_first",
    )(decode_q, prefix)

    send_b = project_fresh(pick, hidden, key_value_weight, key_value_bias, cached)
    path_b = lax.all_to_all(send_b, "group", 0, 0, tiled=True).reshape(-1, 2 * head)

    maximum, total = pl.pallas_call(
        functools.partial(middle_kernel, scale, steps, blocks),
        grid=(blocks + 1,),
        out_shape=state,
        in_specs=[
            spec(decode_q.shape),
            pl.BlockSpec(
                (BLOCK, 2 * head), lambda i: (jnp.minimum(i + FIRST_BLOCKS, all_blocks - 1), 0)
            ),
            spec(path_a.shape),
            spec(bias_a.shape),
            spec(own.shape),
            spec(state[0].shape),
            spec(state[1].shape),
        ],
        out_specs=[spec(s.shape) for s in state],
        scratch_shapes=[query_scratch],
        compiler_params=params,
        cost_estimate=attention_cost(queries, head, blocks * BLOCK + path_a.shape[0]),
        name="attend_middle",
    )(decode_q, prefix, path_a, bias_a, own, maximum, total)

    return pl.pallas_call(
        functools.partial(last_kernel, scale),
        out_shape=jax.ShapeDtypeStruct(decode_q.shape, jnp.bfloat16),
        in_specs=[spec(a.shape) for a in (decode_q, path_b, bias_b) + state],
        out_specs=spec(decode_q.shape),
        scratch_shapes=[
            query_scratch,
            pltpu.VMEM(state[0].shape, jnp.float32),
            pltpu.VMEM(state[1].shape, jnp.float32),
        ],
        compiler_params=params,
        cost_estimate=attention_cost(queries, head, path_b.shape[0]),
        name="attend_last",
    )(decode_q, path_b, bias_b, maximum, total)


def solution(mesh):
    placed = (
        P("tp", None, None),
        P("tp", "group", None, None),
        P(("group", "tp"), None),
        P(None, "tp"),
        P("tp"),
        P("group", "tp"),
        P("tp", "group", None),
        P(),
        P(),
        P(),
    )
    return jax.shard_map(
        per_device, mesh=mesh, in_specs=placed, out_specs=P("group", "tp"), check_vma=False
    )
```

time: 308 us -> 95.6 us (0.31)
  waiting for transfers between devices: 148 us -> 21.3 us
  matrix products: 73.2 us -> 0 us
  Pallas kernels: 0 us -> 41.1 us
  other arithmetic: 34.5 us -> 0 us
  local copies, waits for them, and re-layouts: 36 us -> 9.99 us
  starting transfers between devices: 0.08 us -> 22.6 us
  between operations: 13.7 us -> 0.08 us
    all_gather x2 -> x0, waiting for transfers between devices: 148 us -> none  [the longest x1 91.8 us: per_device(): shard_kv = lax.all_gather(node_lookup_table, 'group', axis=1, tiled=True)]
    dot_general x21 -> x0, matrix products: 73.2 us -> none  [the longest x10 46.9 us: attend(): jnp.einsum('hrk,hkd->hrd', weights.astype(jnp.bfloat16), key_rows[..., he...]
    pallas_call x0 -> x5, Pallas kernels: none -> 41.1 us  [the longest x1 15.5 us: per_device(): pl.pallas_call(functools.partial(middle_kernel, scale, steps, blocks), gr...]
    reduce_sum x76 -> x0, other arithmetic: 27.8 us -> none  [the longest x10 15.8 us: attend(): summed = summed * factor + jnp.sum(weights, axis=-1)]
    while x25 -> x0, local copies, waits for them, and re-layouts: 25.7 us -> none
    all_to_all x0 -> x3, starting transfers between devices: none -> 22.6 us  [the longest x1 8.46 us: per_device(): lax.all_to_all(send_a, 'group', 0, 0, tiled=True).reshape(-1, 2 * head)]
    all_to_all x0 -> x3, waiting for transfers between devices: none -> 21.3 us  [the longest x1 21.3 us: per_device(): lax.all_to_all(jnp.broadcast_to(fresh_hidden[None], (tp,) + fresh_hidden....]
    gather x1 -> x0, local copies, waits for them, and re-layouts: 6.45 us -> none  [per_device(): jnp.take(shard_kv, local_ids, axis=1)]
  transfers between devices with their start and end apart: 2 -> 3, of which waited for: 2 -> 1; matrix products, arithmetic and copies ran while one was open for 6% -> 1% of each run, Pallas kernels for 0% -> 39%
where the time goes in v1:
time: 95.6 us; the launch traced here: 95.1 us
  Pallas kernels  41.1 us (43%)
  starting transfers between devices  22.6 us (24%)
  waiting for transfers between devices  21.3 us (22%)
  local copies, waits for them, and re-layouts  9.99 us (10%)
    all_to_all x1, waiting for transfers between devices, per_device(): lax.all_to_all(jnp.broadcast_to(fresh_hidden[None], (tp,) + fresh_hidden....  21.3 us
    pallas_call x1, Pallas kernels, per_device(): pl.pallas_call(functools.partial(middle_kernel, scale, steps, blocks), gr...  15.5 us
    pallas_call x1, Pallas kernels, per_device(): pl.pallas_call(functools.partial(first_kernel, scale), grid=(FIRST_BLOCKS...  12 us
    all_to_all x1, starting transfers between devices, per_device(): lax.all_to_all(send_a, 'group', 0, 0, tiled=True).reshape(-1, 2 * head)  8.46 us
    all_to_all x1, starting transfers between devices, per_device(): lax.all_to_all(send_b, 'group', 0, 0, tiled=True).reshape(-1, 2 * head)  7.24 us
    all_to_all x1, starting transfers between devices, per_device(): lax.all_to_all(jnp.broadcast_to(fresh_hidden[None], (tp,) + fresh_hidden....  6.91 us
    unnamed x26, local copies, waits for them, and re-layouts  6.26 us
    pallas_call x1, Pallas kernels, project_fresh(): pl.pallas_call(fresh_kernel, grid=(depth // step,), out_shape=jax.ShapeDt...  5.85 us
  transfers between devices with their start and end apart: 3, of which 1 were waited for; matrix products, arithmetic and copies ran while one was open for 1% of the time, Pallas kernels for 39%

profile of v1, /device:TPU:1, one launch (start us, length us, event | category | flops | bytes accessed | tf_op | source)
XLA Modules:
  0.0 95.1 jit_solution(1840775984845319189)
XLA Ops:
  0.0 0.0 copy-start.11
  0.0 2.5 %broadcast_in_dim.5 = bf16[8,16,8192]{2,1,0:T(8,128)(2,1)} broadcast(bf16[16,8192]{1,0:T(8,128)(2,1)} %param.12), dimensions={1,2} | broadcast | bytes 2359296 | tf_op jit(solution)/shard_map/broadcast_in_dim | solution.py:337
  2.5 0.0 copy-start.12
  2.5 6.9 %all-to-all-start = ((bf16[8,16,8192]{2,1,0:T(8,128)(2,1)}), bf16[8,16,8192]{2,1,0:T(8,128)(2,1)S(1)}, u32[]{:S(2)}, u32[]{:S(2)}) async-start(bf16[8,16,8192]{2,1,0:T(8,128)(2,1)} %broadcast_in_dim.5), calls=%async_computation | async-start | bytes 4194304 | tf_op jit(solution)/shard_map/all_to_all | solution.py:336
  9.4 0.0 copy-done.11
  9.4 0.7 broadcast_in_dim.4.child_ref
  10.1 4.1 %route.1 = (s32[16,128]{1,0:T(8,128)}, f32[16,128]{1,0:T(8,128)}, f32[16,128]{1,0:T(8,128)}, bf16[16,2,64,256]{3,2,1,0:T(8,128)(2,1)}) custom-call(s32[4,128]{1,0:T(4,128)} %bitcast.14, s32[16,128]{1,0:T(8,128)} %broadcast_in_dim.4.child_ref, s32[4,128]{1,0:T(4,128)} %bitcast.15, bf16[30,64,256]{2,1,0:T(8,128)(2,1)} %bitcast.12), custom_call_target="tpu_custom_call" | custom-call | tf_op jit(solution)/shard_map/route/pallas_call | solution.py:123
  14.2 21.3 %all-to-all-done = bf16[8,16,8192]{2,1,0:T(8,128)(2,1)S(1)} async-done(((bf16[8,16,8192]{2,1,0:T(8,128)(2,1)}), bf16[8,16,8192]{2,1,0:T(8,128)(2,1)S(1)}, u32[]{:S(2)}, u32[]{:S(2)}) %all-to-all-start) | async-done | bytes 2097184 | tf_op jit(solution)/shard_map/all_to_all | solution.py:336
  35.5 1.3 %copy-done.10 = bf16[8,16,8192]{2,1,0:T(8,128)(2,1)} copy-done((bf16[8,16,8192]{2,1,0:T(8,128)(2,1)}, bf16[8,16,8192]{2,1,0:T(8,128)(2,1)S(1)}, u32[]{:S(2)}) %copy-start.10) | copy-done | bytes 2097176
  36.9 8.5 %all-to-all-start.2 = ((bf16[16,2,64,256]{3,2,1,0:T(8,128)(2,1)}), bf16[16,2,64,256]{3,2,1,0:T(8,128)(2,1)S(1)}, u32[]{:S(2)}, u32[]{:S(2)}) async-start(bf16[16,2,64,256]{3,2,1,0:T(8,128)(2,1)} %get-tuple-element.15), calls=%async_computation.2 | async-start | bytes 2097152 | tf_op jit(solution)/shard_map/all_to_all | solution.py:340
  45.3 0.0 copy-done.12
  45.3 0.6 reshape.23.bias_ref
  45.9 0.0 copy-done
  45.9 12.0 %attend_first.1 = (f32[1024,128]{1,0:T(8,128)S(1)}, f32[1024,256]{1,0:T(8,128)S(1)}) custom-call(bf16[128,1024]{1,0:T(8,128)(2,1)S(1)} %copy-done, bf16[16384,256]{1,0:T(8,128)(2,1)} %bitcast.16), custom_call_target="tpu_custom_call" | custom-call | flops 8589934592 | bytes 4194304 | tf_op jit(solution)/shard_map/attend_first/pallas_call | solution.py:350
  57.9 0.0 copy-start.8
  57.9 0.8 copy-done.8
  58.7 5.9 %fresh.1 = bf16[16,2,64,256]{3,2,1,0:T(8,128)(2,1)} custom-call(s32[16,128]{1,0:T(8,128)} %get-tuple-element.13.pick_ref, bf16[128,8192]{1,0:T(8,128)(2,1)} %bitcast.11, bf16[8192,256]{1,0:T(8,128)(2,1)} %weight_ref.1, bf16[1,256]{1,0:T(2,128)(2,1)} %reshape.23.bias_ref, bf16[30,64,256]{2,1,0:T(8,128)(2,1)} %bitcast.13), custom_call_target="tpu_custom_call" | custom-call | flops 536870912 | bytes 8388608 | tf_op jit(solution)/shard_map/fresh/pallas_call | solution.py:164
  64.6 0.0 all-to-all-done.2
  64.6 0.0 copy-done.6
  64.6 7.2 %all-to-all-start.1 = ((bf16[16,2,64,256]{3,2,1,0:T(8,128)(2,1)}), bf16[16,2,64,256]{3,2,1,0:T(8,128)(2,1)S(1)}, u32[]{:S(2)}, u32[]{:S(2)}) async-start(bf16[16,2,64,256]{3,2,1,0:T(8,128)(2,1)} %fresh.1), calls=%async_computation.1 | async-start | bytes 2097152 | tf_op jit(solution)/shard_map/all_to_all | solution.py:363
  71.8 0.0 copy-done.1
  71.8 0.0 copy-done.3
  71.8 0.0 copy-start.7
  71.9 1.2 %copy-done.7 = f32[1024,256]{1,0:T(8,128)S(1)} copy-done((f32[1024,256]{1,0:T(8,128)S(1)}, f32[1024,256]{1,0:T(8,128)}, u32[]{:S(2)}) %copy-start.7) | copy-done | bytes 1048600
  73.1 1.0 %copy-done.9 = f32[1024,128]{1,0:T(8,128)S(1)} copy-done((f32[1024,128]{1,0:T(8,128)S(1)}, f32[1024,128]{1,0:T(8,128)}, u32[]{:S(2)}) %copy-start.9) | copy-done | bytes 524312
  74.1 15.5 %attend_middle.1 = (f32[1024,128]{1,0:T(8,128)S(1)}, f32[1024,256]{1,0:T(8,128)S(1)}) custom-call(bf16[128,1024]{1,0:T(8,128)(2,1)S(1)} %copy-done, bf16[16384,256]{1,0:T(8,128)(2,1)} %bitcast.17, bf16[2048,256]{1,0:T(8,128)(2,1)S(1)} %bitcast.8, f32[16,128]{1,0:T(8,128)S(1)} %copy-done.3, bf16[128,256]{1,0:T(8,128)(2,1)S(1)} %bitcast.10, ...), custom_call_target="tpu_custom_call" | custom-call | flops 10737418240 | bytes 5242880 | tf_op jit(solution)/shard_map/attend_middle/pallas_call | solution.py:365
  89.6 0.0 copy-start.4
  89.6 0.8 copy-done.4
  90.4 0.0 all-to-all-done.1
  90.4 0.0 copy-done.2
  90.4 1.0 %copy-done.5 = f32[1024,128]{1,0:T(8,128)S(1)} copy-done((f32[1024,128]{1,0:T(8,128)S(1)}, f32[1024,128]{1,0:T(8,128)}, u32[]{:S(2)}) %copy-start.5) | copy-done | bytes 524312
  91.5 3.6 %attend_last.1 = bf16[128,1024]{1,0:T(8,128)(2,1)} custom-call(bf16[128,1024]{1,0:T(8,128)(2,1)S(1)} %copy-done, bf16[2048,256]{1,0:T(8,128)(2,1)S(1)} %bitcast.9, f32[16,128]{1,0:T(8,128)S(1)} %copy-done.2, f32[1024,128]{1,0:T(8,128)S(1)} %copy-done.5, f32[1024,256]{1,0:T(8,128)S(1)} %get-tuple-element.20.total_in), custom_call_target="tpu_custom_call" | custom-call | flops 2147483648 | bytes 1048576 | tf_op jit(solution)/shard_map/attend_last/pallas_call | solution.py:387
  (8 shorter events, 0.0 us)
Async XLA Ops:
  0.0 9.4 %copy-start.11 = (s32[16]{0:T(128)S(1)}, s32[16]{0:T(128)}, u32[]{:S(2)}) copy-start(s32[16]{0:T(128)} %param.18) | copy-start | bytes 196
  2.5 42.8 %copy-start.12 = (bf16[256]{0:T(256)(128)(2,1)S(1)}, bf16[256]{0:T(256)(128)(2,1)}, u32[]{:S(2)}) copy-start(bf16[256]{0:T(256)(128)(2,1)} %param.14) | copy-start | bytes 1540
  2.5 43.4 %copy-start = (bf16[128,1024]{1,0:T(8,128)(2,1)S(1)}, bf16[128,1024]{1,0:T(8,128)(2,1)}, u32[]{:S(2)}) copy-start(bf16[128,1024]{1,0:T(8,128)(2,1)} %q_ref.5) | copy-start | bytes 786436
  2.5 33.0 %all-to-all-start = ((bf16[8,16,8192]{2,1,0:T(8,128)(2,1)}), bf16[8,16,8192]{2,1,0:T(8,128)(2,1)S(1)}, u32[]{:S(2)}, u32[]{:S(2)}) async-start(bf16[8,16,8192]{2,1,0:T(8,128)(2,1)} %broadcast_in_dim.5), calls=%async_computation | async-start | bytes 4194304 | tf_op jit(solution)/shard_map/all_to_all | solution.py:336
  35.5 1.3 %copy-start.10 = (bf16[8,16,8192]{2,1,0:T(8,128)(2,1)}, bf16[8,16,8192]{2,1,0:T(8,128)(2,1)S(1)}, u32[]{:S(2)}) copy-start(bf16[8,16,8192]{2,1,0:T(8,128)(2,1)S(1)} %all-to-all-done) | copy-start | bytes 6291460
  36.9 27.7 %all-to-all-start.2 = ((bf16[16,2,64,256]{3,2,1,0:T(8,128)(2,1)}), bf16[16,2,64,256]{3,2,1,0:T(8,128)(2,1)S(1)}, u32[]{:S(2)}, u32[]{:S(2)}) async-start(bf16[16,2,64,256]{3,2,1,0:T(8,128)(2,1)} %get-tuple-element.15), calls=%async_computation.2 | async-start | bytes 2097152 | tf_op jit(solution)/shard_map/all_to_all | solution.py:340
  57.9 0.8 copy-start.8
  58.7 5.9 %copy-start.6 = (f32[1024,256]{1,0:T(8,128)}, f32[1024,256]{1,0:T(8,128)S(1)}, u32[]{:S(2)}) copy-start(f32[1024,256]{1,0:T(8,128)S(1)} %get-tuple-element.18.total_in) | copy-start | bytes 3145732
  58.7 13.1 %copy-start.1 = (bf16[1,128,256]{2,1,0:T(8,128)(2,1)S(1)}, bf16[1,128,256]{2,1,0:T(8,128)(2,1)}, u32[]{:S(2)}) copy-start(bf16[1,128,256]{2,1,0:T(8,128)(2,1)} %param.16) | copy-start | bytes 196612
  58.7 13.1 %copy-start.3 = (f32[16,128]{1,0:T(8,128)S(1)}, f32[16,128]{1,0:T(8,128)}, u32[]{:S(2)}) copy-start(f32[16,128]{1,0:T(8,128)} %get-tuple-element.16.bias_ref) | copy-start | bytes 24580
  64.6 25.8 %all-to-all-start.1 = ((bf16[16,2,64,256]{3,2,1,0:T(8,128)(2,1)}), bf16[16,2,64,256]{3,2,1,0:T(8,128)(2,1)S(1)}, u32[]{:S(2)}, u32[]{:S(2)}) async-start(bf16[16,2,64,256]{3,2,1,0:T(8,128)(2,1)} %fresh.1), calls=%async_computation.1 | async-start | bytes 2097152 | tf_op jit(solution)/shard_map/all_to_all | solution.py:363
  71.8 1.2 %copy-start.7 = (f32[1024,256]{1,0:T(8,128)S(1)}, f32[1024,256]{1,0:T(8,128)}, u32[]{:S(2)}) copy-start(f32[1024,256]{1,0:T(8,128)} %copy-done.6) | copy-start | bytes 3145732
  73.1 1.0 %copy-start.9 = (f32[1024,128]{1,0:T(8,128)S(1)}, f32[1024,128]{1,0:T(8,128)}, u32[]{:S(2)}) copy-start(f32[1024,128]{1,0:T(8,128)} %copy-done.8) | copy-start | bytes 1572868
  74.1 16.3 %copy-start.2 = (f32[16,128]{1,0:T(8,128)S(1)}, f32[16,128]{1,0:T(8,128)}, u32[]{:S(2)}) copy-start(f32[16,128]{1,0:T(8,128)} %get-tuple-element.14.bias_ref) | copy-start | bytes 24580
  89.6 0.8 copy-start.4
  90.4 1.0 %copy-start.5 = (f32[1024,128]{1,0:T(8,128)S(1)}, f32[1024,128]{1,0:T(8,128)}, u32[]{:S(2)}) copy-start(f32[1024,128]{1,0:T(8,128)} %copy-done.4) | copy-start | bytes 1572868

commit v2 on v1

--- a/solution.py
+++ b/solution.py
@@ -15,7 +15,8 @@
 FIRST_BLOCKS = 2
 LOW = -1e30
 LOG2E = 1.4426950408889634
-VMEM_LIMIT = 48 * 2**20
+VMEM_LIMIT = 56 * 2**20
+SMALL_LIMIT = 16 * 2**20
 
 
 def spec(shape):
@@ -66,7 +67,10 @@
     none = parent.shape[0] * 128
     jump = jnp.where(parent < 0, none, parent)
     lane = lax.broadcasted_iota(jnp.int32, (groups, width), 1)
-    path = jnp.where(lane == 0, child_ref[...], none)
+    group_row = lax.broadcasted_iota(jnp.int32, (groups, width), 0)
+    path = jnp.full((groups, width), none, jnp.int32)
+    for g in range(groups):
+        path = jnp.where((lane == 0) & (group_row == g), child_ref[g], path)
     reach = 1
     while reach < 64:
         tables = rows_of(jump)
@@ -87,7 +91,6 @@
     pick_ref[...] = pick
     copy = pltpu.make_async_copy(pick_v, pick_s, sem)
     copy.start()
-    group_row = lax.broadcasted_iota(jnp.int32, (groups, width), 0)
     mine = jnp.sum(jnp.where(group_row == me, path, 0).astype(jnp.float32), axis=0, keepdims=True)
     mine = jnp.broadcast_to(mine, (groups, width)).astype(jnp.int32)
     there = mine < none
@@ -109,45 +112,58 @@
 
 def route(parent, child_parent, node_len, cached):
     groups = child_parent.shape[0]
-    nodes, tokens, width = cached.shape
+    _, tokens, width = cached.shape
     rows = parent.shape[0] // 128
     table = jax.ShapeDtypeStruct((groups, 128), jnp.int32)
     bias = jax.ShapeDtypeStruct((groups, 128), jnp.float32)
     out = (table, bias, bias, jax.ShapeDtypeStruct((groups, 2, tokens, width), cached.dtype))
     args = (
         parent.reshape(rows, 128),
-        jnp.broadcast_to(child_parent[:, None], (groups, 128)),
+        child_parent,
         node_len.reshape(rows, 128),
         cached,
     )
     return pl.pallas_call(
         functools.partial(route_kernel, groups),
         out_shape=out,
-        in_specs=[spec(a.shape) for a in args],
+        in_specs=[
+            spec(args[0].shape),
+            pl.BlockSpec(memory_space=pltpu.SMEM),
+            spec(args[2].shape),
+            spec(args[3].shape),
+        ],
         out_specs=[spec(o.shape) for o in out],
         scratch_shapes=[
             pltpu.VMEM((groups, 128), jnp.int32),
             pltpu.SMEM((groups, 128), jnp.int32),
             pltpu.SemaphoreType.DMA,
         ],
+        compiler_params=pltpu.CompilerParams(vmem_limit_bytes=SMALL_LIMIT),
+        cost_estimate=pl.CostEstimate(flops=2**24, bytes_accessed=2**21, transcendentals=0),
         name="route",
     )(*args)
 
 
-def fresh_kernel(pick_ref, hidden_ref, weight_ref, bias_ref, cached_ref, send_ref, total, table):
+def fresh_kernel(parts, pick_ref, *refs):
+    hidden_refs = refs[:parts]
+    weight_ref, bias_ref, cached_ref, send_ref, total, table, hidden = refs[parts:]
     step = pl.program_id(0)
-    cached_nodes, tokens, width = cached_ref.shape
+    me = lax.axis_index("tp")
+    cached_nodes, tokens, _ = cached_ref.shape
 
     @pl.when(step == 0)
     def _():
         total[...] = jnp.zeros_like(total)
         table[:cached_nodes] = cached_ref[...]
 
-    total[...] += jnp.dot(hidden_ref[...], weight_ref[...], preferred_element_type=jnp.float32)
+    for k, ref in enumerate(hidden_refs):
+        block = ref.shape[0]
+        hidden[pl.ds(pl.multiple_of((me ^ k) * block, block), block), :] = ref[...]
+    total[...] += jnp.dot(hidden[...], weight_ref[...], preferred_element_type=jnp.float32)
 
     @pl.when(step == pl.num_programs(0) - 1)
     def _():
-        rows = (total[...] + bias_ref[...].astype(jnp.float32)).astype(jnp.bfloat16)
+        rows = (total[...] + bias_ref[...].astype(jnp.float32)[None, :]).astype(jnp.bfloat16)
         for f in range(FRESH):
             table[cached_nodes + f] = rows[f * tokens : (f + 1) * tokens]
         for g in range(send_ref.shape[0]):
@@ -159,29 +175,32 @@
 def project_fresh(pick, hidden, weight, bias, cached):
     groups = pick.shape[0]
     nodes, tokens, width = cached.shape
-    rows, depth = hidden.shape
+    block, depth = hidden[0].shape
+    rows = block * len(hidden)
     step = 2048
     return pl.pallas_call(
-        fresh_kernel,
+        functools.partial(fresh_kernel, len(hidden)),
         grid=(depth // step,),
         out_shape=jax.ShapeDtypeStruct((groups, 2, tokens, width), cached.dtype),
         in_specs=[
             pl.BlockSpec(memory_space=pltpu.SMEM),
-            pl.BlockSpec((rows, step), lambda i: (0, i)),
+            *[pl.BlockSpec((block, step), lambda i: (0, i)) for _ in hidden],
             pl.BlockSpec((step, width), lambda i: (i, 0)),
-            spec((1, width)),
+            spec((width,)),
             spec(cached.shape),
         ],
         out_specs=spec((groups, 2, tokens, width)),
         scratch_shapes=[
             pltpu.VMEM((rows, width), jnp.float32),
             pltpu.VMEM((nodes + FRESH, tokens, width), cached.dtype),
+            pltpu.VMEM((rows, step), cached.dtype),
         ],
+        compiler_params=pltpu.CompilerParams(vmem_limit_bytes=SMALL_LIMIT),
         cost_estimate=pl.CostEstimate(
             flops=2 * rows * depth * width, bytes_accessed=8 * 2**20, transcendentals=0
         ),
         name="fresh",
-    )(pick, hidden, weight, bias.reshape(1, width), cached)
+    )(pick, *hidden, weight, bias, cached)
 
 
 def take_keys(query, maximum, total, pieces, scale):
@@ -263,39 +282,58 @@
         query[j * rows : (j + 1) * rows, :] = q_ref[:, j * head : (j + 1) * head]
 
 
-def first_kernel(scale, q_ref, prefix_ref, max_ref, total_ref, query):
-    @pl.when(pl.program_id(0) == 0)
+def put_state(maximum, total, stat_ref, acc_ref):
+    head = acc_ref.shape[1]
+    lane = lax.broadcasted_iota(jnp.int32, stat_ref.shape, 1)
+    stat_ref[...] = jnp.where(lane < head // 2, maximum[...], total[:, head:])
+    acc_ref[...] = total[:, :head]
+
+
+def get_state(stat_ref, acc_ref, maximum, total):
+    rows, head = acc_ref.shape
+    maximum[...] = jnp.broadcast_to(stat_ref[:, :1], (rows, head))
+    total[:, :head] = acc_ref[...]
+    total[:, head:] = jnp.broadcast_to(stat_ref[:, head - 1 :], (rows, head))
+
+
+def first_kernel(scale, q_ref, prefix_ref, stat_ref, acc_ref, query, maximum, total):
+    step = pl.program_id(0)
+
+    @pl.when(step == 0)
     def _():
         load_query(q_ref, query)
-        max_ref[...] = jnp.full_like(max_ref, LOW)
-        total_ref[...] = jnp.zeros_like(total_ref)
-
-    take_keys(query, max_ref, total_ref, plain_pieces(prefix_ref), scale)
-
-
-def middle_kernel(scale, steps, blocks, q_ref, prefix_ref, path_ref, bias_ref, own_ref, max_in, total_in, max_ref, total_ref, query):
+        maximum[...] = jnp.full_like(maximum, LOW)
+        total[...] = jnp.zeros_like(total)
+
+    take_keys(query, maximum, total, plain_pieces(prefix_ref), scale)
+
+    @pl.when(step == pl.num_programs(0) - 1)
+    def _():
+        put_state(maximum, total, stat_ref, acc_ref)
+
+
+def middle_kernel(scale, steps, blocks, q_ref, prefix_ref, path_ref, bias_ref, own_ref, stat_in, acc_in, stat_ref, acc_ref, query, maximum, total):
     step = pl.program_id(0)
 
     @pl.when(step == 0)
     def _():
         load_query(q_ref, query)
-        max_ref[...] = max_in[...]
-        total_ref[...] = total_in[...]
+        get_state(stat_in, acc_in, maximum, total)
 
     @pl.when(step < blocks)
     def _():
-        take_keys(query, max_ref, total_ref, plain_pieces(prefix_ref), scale)
+        take_keys(query, maximum, total, plain_pieces(prefix_ref), scale)
 
     @pl.when(step == blocks)
     def _():
         pieces = masked_pieces(path_ref, bias_ref) + own_piece(own_ref, steps)
-        take_keys(query, max_ref, total_ref, pieces, scale)
-
-
-def last_kernel(scale, q_ref, path_ref, bias_ref, max_in, total_in, out_ref, query, maximum, total):
+        take_keys(query, maximum, total, pieces, scale)
+        put_state(maximum, total, stat_ref, acc_ref)
+
+
+def last_kernel(scale, q_ref, path_ref, bias_ref, stat_in, acc_in, out_ref, query, maximum, total):
     load_query(q_ref, query)
-    maximum[...] = max_in[...]
-    total[...] = total_in[...]
+    get_state(stat_in, acc_in, maximum, total)
     take_keys(query, maximum, total, masked_pieces(path_ref, bias_ref), scale)
     rows, head = q_ref.shape[0], query.shape[1]
     for j in range(q_ref.shape[1] // head):
@@ -333,27 +371,28 @@
     queries = rows * (decode_q.shape[1] // head)
     tp = lax.axis_size("tp")
 
-    hidden = lax.all_to_all(
-        jnp.broadcast_to(fresh_hidden[None], (tp,) + fresh_hidden.shape), "tp", 0, 0, tiled=True
-    ).reshape(tp * fresh_hidden.shape[0], fresh_hidden.shape[1])
+    hidden = [fresh_hidden] + [
+        lax.ppermute(fresh_hidden, "tp", [(t, t ^ k) for t in range(tp)]) for k in range(1, tp)
+    ]
     pick, bias_a, bias_b, send_a = route(parent, child_parent, node_len, cached)
     path_a = lax.all_to_all(send_a, "group", 0, 0, tiled=True).reshape(-1, 2 * head)
 
-    state = (
-        jax.ShapeDtypeStruct((queries, 128), jnp.float32),
-        jax.ShapeDtypeStruct((queries, 2 * head), jnp.float32),
-    )
+    state = (jax.ShapeDtypeStruct((queries, head), jnp.float32),) * 2
     params = pltpu.CompilerParams(vmem_limit_bytes=VMEM_LIMIT)
-    query_scratch = pltpu.VMEM((queries, head), jnp.bfloat16)
+    scratch = [
+        pltpu.VMEM((queries, head), jnp.bfloat16),
+        pltpu.VMEM((queries, head), jnp.float32),
+        pltpu.VMEM((queries, 2 * head), jnp.float32),
+    ]
     all_blocks = prefix.shape[0] // BLOCK
     blocks = all_blocks - FIRST_BLOCKS
-    maximum, total = pl.pallas_call(
+    stat, acc = pl.pallas_call(
         functools.partial(first_kernel, scale),
         grid=(FIRST_BLOCKS,),
         out_shape=state,
         in_specs=[spec(decode_q.shape), pl.BlockSpec((BLOCK, 2 * head), lambda i: (i, 0))],
         out_specs=[spec(s.shape) for s in state],
-        scratch_shapes=[query_scratch],
+        scratch_shapes=scratch,
         compiler_params=params,
         cost_estimate=attention_cost(queries, head, FIRST_BLOCKS * BLOCK),
         name="attend_first",
@@ -362,7 +401,7 @@
     send_b = project_fresh(pick, hidden, key_value_weight, key_value_bias, cached)
     path_b = lax.all_to_all(send_b, "group", 0, 0, tiled=True).reshape(-1, 2 * head)
 
-    maximum, total = pl.pallas_call(
+    stat, acc = pl.pallas_call(
         functools.partial(middle_kernel, scale, steps, blocks),
         grid=(blocks + 1,),
         out_shape=state,
@@ -378,26 +417,22 @@
             spec(state[1].shape),
         ],
         out_specs=[spec(s.shape) for s in state],
-        scratch_shapes=[query_scratch],
+        scratch_shapes=scratch,
         compiler_params=params,
         cost_estimate=attention_cost(queries, head, blocks * BLOCK + path_a.shape[0]),
         name="attend_middle",
-    )(decode_q, prefix, path_a, bias_a, own, maximum, total)
+    )(decode_q, prefix, path_a, bias_a, own, stat, acc)
 
     return pl.pallas_call(
         functools.partial(last_kernel, scale),
         out_shape=jax.ShapeDtypeStruct(decode_q.shape, jnp.bfloat16),
         in_specs=[spec(a.shape) for a in (decode_q, path_b, bias_b) + state],
         out_specs=spec(decode_q.shape),
-        scratch_shapes=[
-            query_scratch,
-            pltpu.VMEM(state[0].shape, jnp.float32),
-            pltpu.VMEM(state[1].shape, jnp.float32),
-        ],
+        scratch_shapes=scratch,
         compiler_params=params,
         cost_estimate=attention_cost(queries, head, path_b.shape[0]),
         name="attend_last",
-    )(decode_q, path_b, bias_b, maximum, total)
+    )(decode_q, path_b, bias_b, stat, acc)
 
 
 def solution(mesh):
@@ -413,6 +448,7 @@
         P(),
         P(),
     )
+
     return jax.shard_map(
         per_device, mesh=mesh, in_specs=placed, out_specs=P("group", "tp"), check_vma=False
     )

time: 95.6 us -> 87 us (0.910)
  waiting for transfers between devices: 21.3 us -> 11.6 us
  local copies, waits for them, and re-layouts: 9.99 us -> 5.41 us
  starting transfers between devices: 22.6 us -> 27.1 us
  Pallas kernels: 41.1 us -> 42.4 us
    all_to_all x1 -> x0, waiting for transfers between devices: 21.3 us -> none  [per_device(): lax.all_to_all(jnp.broadcast_to(fresh_hidden[None], (tp,) + fresh_hidden....]
    ppermute x0 -> x7, waiting for transfers between devices: none -> 11.6 us  [per_device(): lax.ppermute(fresh_hidden, 'tp', [(t, t ^ k) for t in range(tp)])]
    ppermute x0 -> x7, starting transfers between devices: none -> 11.1 us  [per_device(): lax.ppermute(fresh_hidden, 'tp', [(t, t ^ k) for t in range(tp)])]
    all_to_all x1 -> x0, starting transfers between devices: 6.91 us -> none  [per_device(): lax.all_to_all(jnp.broadcast_to(fresh_hidden[None], (tp,) + fresh_hidden....]
    broadcast_in_dim x2 -> x0, local copies, waits for them, and re-layouts: 3.17 us -> none  [the longest x1 2.5 us: per_device(): jnp.broadcast_to(fresh_hidden[None], (tp,) + fresh_hidden.shape)]
    pallas_call x1, Pallas kernels: 5.85 us -> 3.45 us  [project_fresh(): pl.pallas_call(functools.partial(fresh_kernel, len(hidden)), grid=(depth...]
    pallas_call x1, Pallas kernels: 15.5 us -> 17.3 us  [per_device(): pl.pallas_call(functools.partial(middle_kernel, scale, steps, blocks), gr...]
    pallas_call x1, Pallas kernels: 3.59 us -> 5.1 us  [per_device(): pl.pallas_call(functools.partial(last_kernel, scale), out_shape=jax.Shape...]
  transfers between devices with their start and end apart: 3 -> 9, of which waited for: 1 -> 2; matrix products, arithmetic and copies ran while one was open for 1% -> 0% of each run, Pallas kernels for 39% -> 43%
where the time goes in v2:
time: 87 us; the launch traced here: 86.6 us
  Pallas kernels  42.4 us (49%)
  starting transfers between devices  27.1 us (31%)
  waiting for transfers between devices  11.6 us (13%)
  local copies, waits for them, and re-layouts  5.41 us (6%)
    pallas_call x1, Pallas kernels, per_device(): pl.pallas_call(functools.partial(middle_kernel, scale, steps, blocks), gr...  17.3 us
    pallas_call x1, Pallas kernels, per_device(): pl.pallas_call(functools.partial(first_kernel, scale), grid=(FIRST_BLOCKS...  13.2 us
    ppermute x7, waiting for transfers between devices, per_device(): lax.ppermute(fresh_hidden, 'tp', [(t, t ^ k) for t in range(tp)])  11.6 us
    ppermute x7, starting transfers between devices, per_device(): lax.ppermute(fresh_hidden, 'tp', [(t, t ^ k) for t in range(tp)])  11.1 us
    all_to_all x1, starting transfers between devices, per_device(): lax.all_to_all(send_b, 'group', 0, 0, tiled=True).reshape(-1, 2 * head)  8.1 us
    all_to_all x1, starting transfers between devices, per_device(): lax.all_to_all(send_a, 'group', 0, 0, tiled=True).reshape(-1, 2 * head)  7.88 us
    unnamed x22, local copies, waits for them, and re-layouts  5.41 us
    pallas_call x1, Pallas kernels, per_device(): pl.pallas_call(functools.partial(last_kernel, scale), out_shape=jax.Shape...  5.1 us
  transfers between devices with their start and end apart: 9, of which 2 were waited for; matrix products, arithmetic and copies ran while one was open for 0% of the time, Pallas kernels for 43%

profile of v2, /device:TPU:1, one launch (start us, length us, event | category | flops | bytes accessed | tf_op | source)
XLA Modules:
  0.0 86.6 jit_solution(13912164369204756397)
XLA Ops:
  0.0 2.0 %collective-permute-start = (bf16[16,8192]{1,0:T(8,128)(2,1)}, bf16[16,8192]{1,0:T(8,128)(2,1)S(1)}, u32[]{:S(2)}, u32[]{:S(2)}) collective-permute-start(bf16[16,8192]{1,0:T(8,128)(2,1)} %refs_0_.1), channel_id=1, source_target_pairs={{0,1},{1,0},{2,3},{3,2},{4,5},{5,4},{6,7},{7,6},{8,9},{9,8},{10,11... | collective-permute-start | bytes 786440 | tf_op jit(solution)/shard_map/ppermute | solution.py:375
  2.0 1.6 %collective-permute-start.1 = (bf16[16,8192]{1,0:T(8,128)(2,1)}, bf16[16,8192]{1,0:T(8,128)(2,1)S(1)}, u32[]{:S(2)}, u32[]{:S(2)}) collective-permute-start(bf16[16,8192]{1,0:T(8,128)(2,1)} %refs_0_.1), channel_id=1, source_target_pairs={{0,2},{1,3},{2,0},{3,1},{4,6},{5,7},{6,4},{7,5},{8,10},{9,11},{10,... | collective-permute-start | bytes 786440 | tf_op jit(solution)/shard_map/ppermute | solution.py:375
  3.7 1.2 %copy-done.1 = bf16[1,30,64,256]{3,2,1,0:T(8,128)(2,1)S(1)} copy-done((bf16[1,30,64,256]{3,2,1,0:T(8,128)(2,1)S(1)}, bf16[1,30,64,256]{3,2,1,0:T(8,128)(2,1)}, u32[]{:S(2)}) %copy-start.1) | copy-done | bytes 983064
  4.9 0.7 copy-done.4
  5.6 0.7 copy-done.5
  6.2 0.7 copy-done.6
  6.9 3.4 %route.1 = (s32[16,128]{1,0:T(8,128)S(1)}, f32[16,128]{1,0:T(8,128)S(1)}, f32[16,128]{1,0:T(8,128)S(1)}, bf16[16,2,64,256]{3,2,1,0:T(8,128)(2,1)}) custom-call(s32[4,128]{1,0:T(4,128)S(1)} %bitcast.9, s32[16]{0:T(128)S(1)} %copy-done.6, s32[4,128]{1,0:T(4,128)S(1)} %bitcast.10, bf16[30,64,256]{2,1,0:T(8,128)(2,1)S(1)} %bitcast.7), custom_call_target="tpu_custom_call" | custom-call | flops 16777216 | bytes 2097152 | tf_op jit(solution)/shard_map/route/pallas_call | solution.py:126
  10.3 0.6 copy-done.8
  10.9 0.6 copy-done.9
  11.5 7.9 %all-to-all-start.1 = ((bf16[16,2,64,256]{3,2,1,0:T(8,128)(2,1)}), bf16[16,2,64,256]{3,2,1,0:T(8,128)(2,1)}, u32[]{:S(2)}, u32[]{:S(2)}) async-start(bf16[16,2,64,256]{3,2,1,0:T(8,128)(2,1)} %get-tuple-element.15), calls=%async_computation.1 | async-start | bytes 2097152 | tf_op jit(solution)/shard_map/all_to_all | solution.py:378
  19.4 0.0 collective-permute-start.2
  19.4 3.4 %collective-permute-start.3 = (bf16[16,8192]{1,0:T(8,128)(2,1)}, bf16[16,8192]{1,0:T(8,128)(2,1)S(1)}, u32[]{:S(2)}, u32[]{:S(2)}) collective-permute-start(bf16[16,8192]{1,0:T(8,128)(2,1)} %refs_0_.1), channel_id=1, source_target_pairs={{0,4},{1,5},{2,6},{3,7},{4,0},{5,1},{6,2},{7,3},{8,12},{9,13},{10,... | collective-permute-start | bytes 786440 | tf_op jit(solution)/shard_map/ppermute | solution.py:375
  22.8 0.9 %collective-permute-start.4 = (bf16[16,8192]{1,0:T(8,128)(2,1)}, bf16[16,8192]{1,0:T(8,128)(2,1)S(1)}, u32[]{:S(2)}, u32[]{:S(2)}) collective-permute-start(bf16[16,8192]{1,0:T(8,128)(2,1)} %refs_0_.1), channel_id=1, source_target_pairs={{0,5},{1,4},{2,7},{3,6},{4,1},{5,0},{6,3},{7,2},{8,13},{9,12},{10,... | collective-permute-start | bytes 786440 | tf_op jit(solution)/shard_map/ppermute | solution.py:375
  23.7 0.0 collective-permute-done.refs_1_
  23.7 3.1 %collective-permute-start.5 = (bf16[16,8192]{1,0:T(8,128)(2,1)}, bf16[16,8192]{1,0:T(8,128)(2,1)S(1)}, u32[]{:S(2)}, u32[]{:S(2)}) collective-permute-start(bf16[16,8192]{1,0:T(8,128)(2,1)} %refs_0_.1), channel_id=1, source_target_pairs={{0,6},{1,7},{2,4},{3,5},{4,2},{5,3},{6,0},{7,1},{8,14},{9,15},{10,... | collective-permute-start | bytes 786440 | tf_op jit(solution)/shard_map/ppermute | solution.py:375
  26.9 0.0 collective-permute-done.1.refs_2_
  26.9 0.0 collective-permute-start.6
  26.9 0.0 copy-start.2
  26.9 0.0 copy-start.7
  26.9 13.2 %attend_first.1 = (f32[1024,128]{1,0:T(8,128)}, f32[1024,128]{1,0:T(8,128)}) custom-call(bf16[128,1024]{1,0:T(8,128)(2,1)} %q_ref.5, bf16[16384,256]{1,0:T(8,128)(2,1)} %bitcast.12), custom_call_target="tpu_custom_call" | custom-call | flops 8589934592 | bytes 4194304 | tf_op jit(solution)/shard_map/attend_first/pallas_call | solution.py:389
  40.1 0.0 collective-permute-done.2.refs_3_
  40.1 0.0 collective-permute-done.3.refs_4_
  40.1 6.6 %collective-permute-done.4.refs_5_ = bf16[16,8192]{1,0:T(8,128)(2,1)S(1)} collective-permute-done((bf16[16,8192]{1,0:T(8,128)(2,1)}, bf16[16,8192]{1,0:T(8,128)(2,1)S(1)}, u32[]{:S(2)}, u32[]{:S(2)}) %collective-permute-start.4) | collective-permute-done | bytes 262176 | tf_op jit(solution)/shard_map/ppermute | solution.py:375
  46.7 0.0 collective-permute-done.5.refs_6_
  46.7 5.0 %collective-permute-done.6.refs_7_ = bf16[16,8192]{1,0:T(8,128)(2,1)S(1)} collective-permute-done((bf16[16,8192]{1,0:T(8,128)(2,1)}, bf16[16,8192]{1,0:T(8,128)(2,1)S(1)}, u32[]{:S(2)}, u32[]{:S(2)}) %collective-permute-start.6) | collective-permute-done | bytes 262176 | tf_op jit(solution)/shard_map/ppermute | solution.py:375
  51.7 3.4 %fresh.1 = bf16[16,2,64,256]{3,2,1,0:T(8,128)(2,1)} custom-call(s32[16,128]{1,0:T(8,128)S(1)} %get-tuple-element.13.pick_ref, bf16[16,8192]{1,0:T(8,128)(2,1)S(1)} %copy-done.3, bf16[16,8192]{1,0:T(8,128)(2,1)S(1)} %collective-permute-done.refs_1_, bf16[16,8192]{1,0:T(8,128)(2,1)S(1)} %collective-permute-done.1.refs_2_, ...), custom_call_target="tpu_custom_call" | custom-call | flops 536870912 | bytes 8388608 | tf_op jit(solution)/shard_map/fresh/pallas_call | solution.py:181
  55.1 0.0 all-to-all-done.1
  55.1 8.1 %all-to-all-start = ((bf16[16,2,64,256]{3,2,1,0:T(8,128)(2,1)}), bf16[16,2,64,256]{3,2,1,0:T(8,128)(2,1)S(1)}, u32[]{:S(2)}, u32[]{:S(2)}) async-start(bf16[16,2,64,256]{3,2,1,0:T(8,128)(2,1)} %fresh.1), calls=%async_computation | async-start | bytes 2097152 | tf_op jit(solution)/shard_map/all_to_all | solution.py:402
  63.2 17.3 %attend_middle.1 = (f32[1024,128]{1,0:T(8,128)}, f32[1024,128]{1,0:T(8,128)}) custom-call(bf16[128,1024]{1,0:T(8,128)(2,1)} %q_ref.5, bf16[16384,256]{1,0:T(8,128)(2,1)} %bitcast.13, bf16[2048,256]{1,0:T(8,128)(2,1)} %bitcast.5.path_ref, f32[16,128]{1,0:T(8,128)} %copy-done.9, bf16[128,256]{1,0:T(8,128)(2,1)} %bitcast.14, ...), custom_call_target="tpu_custom_call" | custom-call | flops 10737418240 | bytes 5242880 | tf_op jit(solution)/shard_map/attend_middle/pallas_call | solution.py:404
  80.5 0.0 all-to-all-done
  80.5 1.0 %copy-done.10 = bf16[16,2,64,256]{3,2,1,0:T(8,128)(2,1)} copy-done((bf16[16,2,64,256]{3,2,1,0:T(8,128)(2,1)}, bf16[16,2,64,256]{3,2,1,0:T(8,128)(2,1)S(1)}, u32[]{:S(2)}) %copy-start.10) | copy-done | bytes 1048600
  81.5 5.1 %attend_last.1 = bf16[128,1024]{1,0:T(8,128)(2,1)} custom-call(bf16[128,1024]{1,0:T(8,128)(2,1)} %q_ref.5, bf16[2048,256]{1,0:T(8,128)(2,1)} %bitcast.11, f32[16,128]{1,0:T(8,128)} %copy-done.8, f32[1024,128]{1,0:T(8,128)} %get-tuple-element.19.stat_in, f32[1024,128]{1,0:T(8,128)} %get-tuple-element.20.acc_in), custom_call_target="tpu_custom_call" | custom-call | flops 2147483648 | bytes 1048576 | tf_op jit(solution)/shard_map/attend_last/pallas_call | solution.py:426
  (13 shorter events, 0.0 us)
Async XLA Ops:
  0.0 23.7 %collective-permute-start = (bf16[16,8192]{1,0:T(8,128)(2,1)}, bf16[16,8192]{1,0:T(8,128)(2,1)S(1)}, u32[]{:S(2)}, u32[]{:S(2)}) collective-permute-start(bf16[16,8192]{1,0:T(8,128)(2,1)} %refs_0_.1), channel_id=1, source_target_pairs={{0,1},{1,0},{2,3},{3,2},{4,5},{5,4},{6,7},{7,6},{8,9},{9,8},{10,11... | collective-permute-start | bytes 786440 | tf_op jit(solution)/shard_map/ppermute | solution.py:375
  2.0 24.8 %collective-permute-start.1 = (bf16[16,8192]{1,0:T(8,128)(2,1)}, bf16[16,8192]{1,0:T(8,128)(2,1)S(1)}, u32[]{:S(2)}, u32[]{:S(2)}) collective-permute-start(bf16[16,8192]{1,0:T(8,128)(2,1)} %refs_0_.1), channel_id=1, source_target_pairs={{0,2},{1,3},{2,0},{3,1},{4,6},{5,7},{6,4},{7,5},{8,10},{9,11},{10,... | collective-permute-start | bytes 786440 | tf_op jit(solution)/shard_map/ppermute | solution.py:375
  3.7 1.2 %copy-start.1 = (bf16[1,30,64,256]{3,2,1,0:T(8,128)(2,1)S(1)}, bf16[1,30,64,256]{3,2,1,0:T(8,128)(2,1)}, u32[]{:S(2)}) copy-start(bf16[1,30,64,256]{3,2,1,0:T(8,128)(2,1)} %param.11) | copy-start | bytes 2949124
  4.9 0.7 copy-start.4
  5.6 0.7 copy-start.5
  6.2 0.7 copy-start.6
  10.3 0.6 copy-start.8
  10.9 0.6 copy-start.9
  11.5 43.6 %all-to-all-start.1 = ((bf16[16,2,64,256]{3,2,1,0:T(8,128)(2,1)}), bf16[16,2,64,256]{3,2,1,0:T(8,128)(2,1)}, u32[]{:S(2)}, u32[]{:S(2)}) async-start(bf16[16,2,64,256]{3,2,1,0:T(8,128)(2,1)} %get-tuple-element.15), calls=%async_computation.1 | async-start | bytes 2097152 | tf_op jit(solution)/shard_map/all_to_all | solution.py:378
  19.4 20.7 %collective-permute-start.2 = (bf16[16,8192]{1,0:T(8,128)(2,1)}, bf16[16,8192]{1,0:T(8,128)(2,1)S(1)}, u32[]{:S(2)}, u32[]{:S(2)}) collective-permute-start(bf16[16,8192]{1,0:T(8,128)(2,1)} %refs_0_.1), channel_id=1, source_target_pairs={{0,3},{1,2},{2,1},{3,0},{4,7},{5,6},{6,5},{7,4},{8,11},{9,10},{10,... | collective-permute-start | bytes 786440 | tf_op jit(solution)/shard_map/ppermute | solution.py:375
  19.4 20.7 %collective-permute-start.3 = (bf16[16,8192]{1,0:T(8,128)(2,1)}, bf16[16,8192]{1,0:T(8,128)(2,1)S(1)}, u32[]{:S(2)}, u32[]{:S(2)}) collective-permute-start(bf16[16,8192]{1,0:T(8,128)(2,1)} %refs_0_.1), channel_id=1, source_target_pairs={{0,4},{1,5},{2,6},{3,7},{4,0},{5,1},{6,2},{7,3},{8,12},{9,13},{10,... | collective-permute-start | bytes 786440 | tf_op jit(solution)/shard_map/ppermute | solution.py:375
  22.8 23.9 %collective-permute-start.4 = (bf16[16,8192]{1,0:T(8,128)(2,1)}, bf16[16,8192]{1,0:T(8,128)(2,1)S(1)}, u32[]{:S(2)}, u32[]{:S(2)}) collective-permute-start(bf16[16,8192]{1,0:T(8,128)(2,1)} %refs_0_.1), channel_id=1, source_target_pairs={{0,5},{1,4},{2,7},{3,6},{4,1},{5,0},{6,3},{7,2},{8,13},{9,12},{10,... | collective-permute-start | bytes 786440 | tf_op jit(solution)/shard_map/ppermute | solution.py:375
  23.7 22.9 %collective-permute-start.5 = (bf16[16,8192]{1,0:T(8,128)(2,1)}, bf16[16,8192]{1,0:T(8,128)(2,1)S(1)}, u32[]{:S(2)}, u32[]{:S(2)}) collective-permute-start(bf16[16,8192]{1,0:T(8,128)(2,1)} %refs_0_.1), channel_id=1, source_target_pairs={{0,6},{1,7},{2,4},{3,5},{4,2},{5,3},{6,0},{7,1},{8,14},{9,15},{10,... | collective-permute-start | bytes 786440 | tf_op jit(solution)/shard_map/ppermute | solution.py:375
  26.9 24.8 %collective-permute-start.6 = (bf16[16,8192]{1,0:T(8,128)(2,1)}, bf16[16,8192]{1,0:T(8,128)(2,1)S(1)}, u32[]{:S(2)}, u32[]{:S(2)}) collective-permute-start(bf16[16,8192]{1,0:T(8,128)(2,1)} %refs_0_.1), channel_id=1, source_target_pairs={{0,7},{1,6},{2,5},{3,4},{4,3},{5,2},{6,1},{7,0},{8,15},{9,14},{10,... | collective-permute-start | bytes 786440 | tf_op jit(solution)/shard_map/ppermute | solution.py:375
  26.9 24.8 %copy-start = (bf16[8192,256]{1,0:T(8,128)(2,1)S(1)}, bf16[8192,256]{1,0:T(8,128)(2,1)}, u32[]{:S(2)}) copy-start(bf16[8192,256]{1,0:T(8,128)(2,1)} %refs_8_.1) | copy-start | bytes 12582916
  26.9 24.8 %copy-start.2 = (bf16[1,30,64,256]{3,2,1,0:T(8,128)(2,1)S(1)}, bf16[1,30,64,256]{3,2,1,0:T(8,128)(2,1)}, u32[]{:S(2)}) copy-start(bf16[1,30,64,256]{3,2,1,0:T(8,128)(2,1)} %param.11) | copy-start | bytes 2949124
  26.9 24.8 %copy-start.3 = (bf16[16,8192]{1,0:T(8,128)(2,1)S(1)}, bf16[16,8192]{1,0:T(8,128)(2,1)}, u32[]{:S(2)}) copy-start(bf16[16,8192]{1,0:T(8,128)(2,1)} %refs_0_.1) | copy-start | bytes 786436
  26.9 24.8 %copy-start.7 = (bf16[256]{0:T(256)(128)(2,1)S(1)}, bf16[256]{0:T(256)(128)(2,1)}, u32[]{:S(2)}) copy-start(bf16[256]{0:T(256)(128)(2,1)} %refs_9_.1) | copy-start | bytes 1540
  55.1 25.4 %all-to-all-start = ((bf16[16,2,64,256]{3,2,1,0:T(8,128)(2,1)}), bf16[16,2,64,256]{3,2,1,0:T(8,128)(2,1)S(1)}, u32[]{:S(2)}, u32[]{:S(2)}) async-start(bf16[16,2,64,256]{3,2,1,0:T(8,128)(2,1)} %fresh.1), calls=%async_computation | async-start | bytes 2097152 | tf_op jit(solution)/shard_map/all_to_all | solution.py:402
  80.5 1.0 %copy-start.10 = (bf16[16,2,64,256]{3,2,1,0:T(8,128)(2,1)}, bf16[16,2,64,256]{3,2,1,0:T(8,128)(2,1)S(1)}, u32[]{:S(2)}) copy-start(bf16[16,2,64,256]{3,2,1,0:T(8,128)(2,1)S(1)} %all-to-all-done) | copy-start | bytes 3145732

commit v3 on v2

--- a/solution.py
+++ b/solution.py
@@ -138,7 +138,6 @@
             pltpu.SMEM((groups, 128), jnp.int32),
             pltpu.SemaphoreType.DMA,
         ],
-        compiler_params=pltpu.CompilerParams(vmem_limit_bytes=SMALL_LIMIT),
         cost_estimate=pl.CostEstimate(flops=2**24, bytes_accessed=2**21, transcendentals=0),
         name="route",
     )(*args)
@@ -384,6 +383,7 @@
         pltpu.VMEM((queries, head), jnp.float32),
         pltpu.VMEM((queries, 2 * head), jnp.float32),
     ]
+    prefix = pltpu.with_memory_space_constraint(prefix, pltpu.HBM)
     all_blocks = prefix.shape[0] // BLOCK
     blocks = all_blocks - FIRST_BLOCKS
     stat, acc = pl.pallas_call(
@@ -400,6 +400,7 @@
 
     send_b = project_fresh(pick, hidden, key_value_weight, key_value_bias, cached)
     path_b = lax.all_to_all(send_b, "group", 0, 0, tiled=True).reshape(-1, 2 * head)
+    path_b = pltpu.with_memory_space_constraint(path_b, pltpu.VMEM)
 
     stat, acc = pl.pallas_call(
         functools.partial(middle_kernel, scale, steps, blocks),
@@ -426,7 +427,13 @@
     return pl.pallas_call(
         functools.partial(last_kernel, scale),
         out_shape=jax.ShapeDtypeStruct(decode_q.shape, jnp.bfloat16),
-        in_specs=[spec(a.shape) for a in (decode_q, path_b, bias_b) + state],
+        in_specs=[
+            spec(decode_q.shape),
+            pl.BlockSpec(memory_space=pltpu.VMEM),
+            spec(bias_b.shape),
+            spec(state[0].shape),
+            spec(state[1].shape),
+        ],
         out_specs=spec(decode_q.shape),
         scratch_shapes=scratch,
         compiler_params=params,

time: 87 us -> 81.9 us (0.941)
  local copies, waits for them, and re-layouts: 5.41 us -> 0.03 us
    unnamed x22 -> x10, local copies, waits for them, and re-layouts: 5.41 us -> 0.03 us
  transfers between devices with their start and end apart: 9 -> 9, of which waited for: 2 -> 2; matrix products, arithmetic and copies ran while one was open for 0% -> 0% of each run, Pallas kernels for 43% -> 47%
where the time goes in v3:
time: 81.9 us; the launch traced here: 81.6 us
  Pallas kernels  42.9 us (52%)
  starting transfers between devices  27.1 us (33%)
  waiting for transfers between devices  11.5 us (14%)
    pallas_call x1, Pallas kernels, per_device(): pl.pallas_call(functools.partial(middle_kernel, scale, steps, blocks), gr...  17.3 us
    pallas_call x1, Pallas kernels, per_device(): pl.pallas_call(functools.partial(first_kernel, scale), grid=(FIRST_BLOCKS...  13.2 us
    ppermute x7, waiting for transfers between devices, per_device(): lax.ppermute(fresh_hidden, 'tp', [(t, t ^ k) for t in range(tp)])  11.5 us
    ppermute x7, starting transfers between devices, per_device(): lax.ppermute(fresh_hidden, 'tp', [(t, t ^ k) for t in range(tp)])  11.1 us
    all_to_all x1, starting transfers between devices, per_device(): lax.all_to_all(send_b, 'group', 0, 0, tiled=True).reshape(-1, 2 * head)  8.06 us
    all_to_all x1, starting transfers between devices, per_device(): lax.all_to_all(send_a, 'group', 0, 0, tiled=True).reshape(-1, 2 * head)  7.9 us
    pallas_call x1, Pallas kernels, per_device(): pl.pallas_call(functools.partial(last_kernel, scale), out_shape=jax.Shape...  4.8 us
    pallas_call x1, Pallas kernels, route(): pl.pallas_call(functools.partial(route_kernel, groups), out_shape=out, in...  4.12 us
  transfers between devices with their start and end apart: 9, of which 2 were waited for; matrix products, arithmetic and copies ran while one was open for 0% of the time, Pallas kernels for 47%

profile of v3, /device:TPU:1, one launch (start us, length us, event | category | flops | bytes accessed | tf_op | source)
XLA Modules:
  0.0 81.6 jit_solution(1891690222758681377)
XLA Ops:
  0.0 2.0 %collective-permute-start = (bf16[16,8192]{1,0:T(8,128)(2,1)}, bf16[16,8192]{1,0:T(8,128)(2,1)S(1)}, u32[]{:S(2)}, u32[]{:S(2)}) collective-permute-start(bf16[16,8192]{1,0:T(8,128)(2,1)} %refs_0_.1), channel_id=1, source_target_pairs={{0,1},{1,0},{2,3},{3,2},{4,5},{5,4},{6,7},{7,6},{8,9},{9,8},{10,11... | collective-permute-start | bytes 786440 | tf_op jit(solution)/shard_map/ppermute | solution.py:374
  2.0 1.6 %collective-permute-start.1 = (bf16[16,8192]{1,0:T(8,128)(2,1)}, bf16[16,8192]{1,0:T(8,128)(2,1)S(1)}, u32[]{:S(2)}, u32[]{:S(2)}) collective-permute-start(bf16[16,8192]{1,0:T(8,128)(2,1)} %refs_0_.1), channel_id=1, source_target_pairs={{0,2},{1,3},{2,0},{3,1},{4,6},{5,7},{6,4},{7,5},{8,10},{9,11},{10,... | collective-permute-start | bytes 786440 | tf_op jit(solution)/shard_map/ppermute | solution.py:374
  3.7 4.1 %route.1 = (s32[16,128]{1,0:T(8,128)}, f32[16,128]{1,0:T(8,128)}, f32[16,128]{1,0:T(8,128)}, bf16[16,2,64,256]{3,2,1,0:T(8,128)(2,1)}) custom-call(s32[4,128]{1,0:T(4,128)} %bitcast.10, s32[16]{0:T(128)} %child_ref.1, s32[4,128]{1,0:T(4,128)} %bitcast.11, bf16[30,64,256]{2,1,0:T(8,128)(2,1)} %bitcast.7), custom_call_target="tpu_custom_call" | custom-call | flops 16777216 | bytes 2097152 | tf_op jit(solution)/shard_map/route/pallas_call | solution.py:126
  7.8 7.9 %all-to-all-start.1 = ((bf16[16,2,64,256]{3,2,1,0:T(8,128)(2,1)}), bf16[16,2,64,256]{3,2,1,0:T(8,128)(2,1)}, u32[]{:S(2)}, u32[]{:S(2)}) async-start(bf16[16,2,64,256]{3,2,1,0:T(8,128)(2,1)} %get-tuple-element.15), calls=%async_computation.1 | async-start | bytes 2097152 | tf_op jit(solution)/shard_map/all_to_all | solution.py:377
  15.7 0.0 collective-permute-start.2
  15.7 3.4 %collective-permute-start.3 = (bf16[16,8192]{1,0:T(8,128)(2,1)}, bf16[16,8192]{1,0:T(8,128)(2,1)S(1)}, u32[]{:S(2)}, u32[]{:S(2)}) collective-permute-start(bf16[16,8192]{1,0:T(8,128)(2,1)} %refs_0_.1), channel_id=1, source_target_pairs={{0,4},{1,5},{2,6},{3,7},{4,0},{5,1},{6,2},{7,3},{8,12},{9,13},{10,... | collective-permute-start | bytes 786440 | tf_op jit(solution)/shard_map/ppermute | solution.py:374
  19.1 0.9 %collective-permute-start.4 = (bf16[16,8192]{1,0:T(8,128)(2,1)}, bf16[16,8192]{1,0:T(8,128)(2,1)S(1)}, u32[]{:S(2)}, u32[]{:S(2)}) collective-permute-start(bf16[16,8192]{1,0:T(8,128)(2,1)} %refs_0_.1), channel_id=1, source_target_pairs={{0,5},{1,4},{2,7},{3,6},{4,1},{5,0},{6,3},{7,2},{8,13},{9,12},{10,... | collective-permute-start | bytes 786440 | tf_op jit(solution)/shard_map/ppermute | solution.py:374
  20.0 0.0 collective-permute-done.refs_1_
  20.0 3.1 %collective-permute-start.5 = (bf16[16,8192]{1,0:T(8,128)(2,1)}, bf16[16,8192]{1,0:T(8,128)(2,1)S(1)}, u32[]{:S(2)}, u32[]{:S(2)}) collective-permute-start(bf16[16,8192]{1,0:T(8,128)(2,1)} %refs_0_.1), channel_id=1, source_target_pairs={{0,6},{1,7},{2,4},{3,5},{4,2},{5,3},{6,0},{7,1},{8,14},{9,15},{10,... | collective-permute-start | bytes 786440 | tf_op jit(solution)/shard_map/ppermute | solution.py:374
  23.2 0.0 collective-permute-done.1.refs_2_
  23.2 0.0 collective-permute-start.6
  23.2 0.0 copy-start.1
  23.2 0.0 copy-start.2
  23.2 0.0 copy-start.3
  23.2 0.0 copy-start.4
  23.2 13.2 %attend_first.1 = (f32[1024,128]{1,0:T(8,128)}, f32[1024,128]{1,0:T(8,128)}) custom-call(bf16[128,1024]{1,0:T(8,128)(2,1)} %q_ref.5, bf16[16384,256]{1,0:T(8,128)(2,1)} %bitcast.12), custom_call_target="tpu_custom_call" | custom-call | flops 8589934592 | bytes 4194304 | tf_op jit(solution)/shard_map/attend_first/pallas_call | solution.py:389
  36.4 0.0 collective-permute-done.2.refs_3_
  36.4 0.0 collective-permute-done.3.refs_4_
  36.4 6.5 %collective-permute-done.4.refs_5_ = bf16[16,8192]{1,0:T(8,128)(2,1)S(1)} collective-permute-done((bf16[16,8192]{1,0:T(8,128)(2,1)}, bf16[16,8192]{1,0:T(8,128)(2,1)S(1)}, u32[]{:S(2)}, u32[]{:S(2)}) %collective-permute-start.4) | collective-permute-done | bytes 262176 | tf_op jit(solution)/shard_map/ppermute | solution.py:374
  43.0 0.0 collective-permute-done.5.refs_6_
  43.0 5.0 %collective-permute-done.6.refs_7_ = bf16[16,8192]{1,0:T(8,128)(2,1)S(1)} collective-permute-done((bf16[16,8192]{1,0:T(8,128)(2,1)}, bf16[16,8192]{1,0:T(8,128)(2,1)S(1)}, u32[]{:S(2)}, u32[]{:S(2)}) %collective-permute-start.6) | collective-permute-done | bytes 262176 | tf_op jit(solution)/shard_map/ppermute | solution.py:374
  47.9 0.0 copy-done
  47.9 0.0 copy-done.1
  48.0 0.0 copy-done.2
  48.0 0.0 copy-done.3
  48.0 0.0 copy-done.4
  48.0 3.5 %fresh.1 = bf16[16,2,64,256]{3,2,1,0:T(8,128)(2,1)} custom-call(s32[16,128]{1,0:T(8,128)S(1)} %copy-done.3, bf16[16,8192]{1,0:T(8,128)(2,1)S(1)} %copy-done.2, bf16[16,8192]{1,0:T(8,128)(2,1)S(1)} %collective-permute-done.refs_1_, bf16[16,8192]{1,0:T(8,128)(2,1)S(1)} %collective-permute-done.1.refs_2_, bf16[16,8192]{1,0:T(8,128)(2,1)S(1)} %collective-permute-done.2.refs_3_, ...), custom_call_target="tpu_custom_call" | custom-call | flops 536870912 | bytes 8388608 | tf_op jit(solution)/shard_map/fresh/pallas_call | solution.py:180
  51.5 0.0 all-to-all-done.1
  51.5 8.1 %all-to-all-start = ((bf16[16,2,64,256]{3,2,1,0:T(8,128)(2,1)}), bf16[16,2,64,256]{3,2,1,0:T(8,128)(2,1)S(1)}, u32[]{:S(2)}, u32[]{:S(2)}) async-start(bf16[16,2,64,256]{3,2,1,0:T(8,128)(2,1)} %fresh.1), calls=%async_computation | async-start | bytes 2097152 | tf_op jit(solution)/shard_map/all_to_all | solution.py:402
  59.5 17.3 %attend_middle.1 = (f32[1024,128]{1,0:T(8,128)}, f32[1024,128]{1,0:T(8,128)}) custom-call(bf16[128,1024]{1,0:T(8,128)(2,1)} %q_ref.5, bf16[16384,256]{1,0:T(8,128)(2,1)} %bitcast.13, bf16[2048,256]{1,0:T(8,128)(2,1)} %bitcast.5.path_ref, f32[16,128]{1,0:T(8,128)} %get-tuple-element.16.bias_ref, bf16[128,256]{1,0:T(8,128)(2,1)} %bitcast.14, ...), custom_call_target="tpu_custom_call" | custom-call | flops 10737418240 | bytes 5242880 | tf_op jit(solution)/shard_map/attend_middle/pallas_call | solution.py:405
  76.8 0.0 all-to-all-done
  76.8 4.8 %attend_last.1 = bf16[128,1024]{1,0:T(8,128)(2,1)} custom-call(bf16[128,1024]{1,0:T(8,128)(2,1)} %q_ref.5, bf16[2048,256]{1,0:T(8,128)(2,1)S(1)} %bitcast.9, f32[16,128]{1,0:T(8,128)} %get-tuple-element.14.bias_ref, f32[1024,128]{1,0:T(8,128)} %get-tuple-element.19.stat_in, f32[1024,128]{1,0:T(8,128)} %get-tuple-element.20.acc_in), custom_call_target="tpu_custom_call" | custom-call | flops 2147483648 | bytes 1048576 | tf_op jit(solution)/shard_map/attend_last/pallas_call | solution.py:427
  (1 shorter events, 0.0 us)
Async XLA Ops:
  0.0 20.0 %collective-permute-start = (bf16[16,8192]{1,0:T(8,128)(2,1)}, bf16[16,8192]{1,0:T(8,128)(2,1)S(1)}, u32[]{:S(2)}, u32[]{:S(2)}) collective-permute-start(bf16[16,8192]{1,0:T(8,128)(2,1)} %refs_0_.1), channel_id=1, source_target_pairs={{0,1},{1,0},{2,3},{3,2},{4,5},{5,4},{6,7},{7,6},{8,9},{9,8},{10,11... | collective-permute-start | bytes 786440 | tf_op jit(solution)/shard_map/ppermute | solution.py:374
  2.0 21.1 %collective-permute-start.1 = (bf16[16,8192]{1,0:T(8,128)(2,1)}, bf16[16,8192]{1,0:T(8,128)(2,1)S(1)}, u32[]{:S(2)}, u32[]{:S(2)}) collective-permute-start(bf16[16,8192]{1,0:T(8,128)(2,1)} %refs_0_.1), channel_id=1, source_target_pairs={{0,2},{1,3},{2,0},{3,1},{4,6},{5,7},{6,4},{7,5},{8,10},{9,11},{10,... | collective-permute-start | bytes 786440 | tf_op jit(solution)/shard_map/ppermute | solution.py:374
  7.8 43.7 %all-to-all-start.1 = ((bf16[16,2,64,256]{3,2,1,0:T(8,128)(2,1)}), bf16[16,2,64,256]{3,2,1,0:T(8,128)(2,1)}, u32[]{:S(2)}, u32[]{:S(2)}) async-start(bf16[16,2,64,256]{3,2,1,0:T(8,128)(2,1)} %get-tuple-element.15), calls=%async_computation.1 | async-start | bytes 2097152 | tf_op jit(solution)/shard_map/all_to_all | solution.py:377
  15.7 20.7 %collective-permute-start.2 = (bf16[16,8192]{1,0:T(8,128)(2,1)}, bf16[16,8192]{1,0:T(8,128)(2,1)S(1)}, u32[]{:S(2)}, u32[]{:S(2)}) collective-permute-start(bf16[16,8192]{1,0:T(8,128)(2,1)} %refs_0_.1), channel_id=1, source_target_pairs={{0,3},{1,2},{2,1},{3,0},{4,7},{5,6},{6,5},{7,4},{8,11},{9,10},{10,... | collective-permute-start | bytes 786440 | tf_op jit(solution)/shard_map/ppermute | solution.py:374
  15.7 20.7 %collective-permute-start.3 = (bf16[16,8192]{1,0:T(8,128)(2,1)}, bf16[16,8192]{1,0:T(8,128)(2,1)S(1)}, u32[]{:S(2)}, u32[]{:S(2)}) collective-permute-start(bf16[16,8192]{1,0:T(8,128)(2,1)} %refs_0_.1), channel_id=1, source_target_pairs={{0,4},{1,5},{2,6},{3,7},{4,0},{5,1},{6,2},{7,3},{8,12},{9,13},{10,... | collective-permute-start | bytes 786440 | tf_op jit(solution)/shard_map/ppermute | solution.py:374
  19.1 23.9 %collective-permute-start.4 = (bf16[16,8192]{1,0:T(8,128)(2,1)}, bf16[16,8192]{1,0:T(8,128)(2,1)S(1)}, u32[]{:S(2)}, u32[]{:S(2)}) collective-permute-start(bf16[16,8192]{1,0:T(8,128)(2,1)} %refs_0_.1), channel_id=1, source_target_pairs={{0,5},{1,4},{2,7},{3,6},{4,1},{5,0},{6,3},{7,2},{8,13},{9,12},{10,... | collective-permute-start | bytes 786440 | tf_op jit(solution)/shard_map/ppermute | solution.py:374
  20.0 22.9 %collective-permute-start.5 = (bf16[16,8192]{1,0:T(8,128)(2,1)}, bf16[16,8192]{1,0:T(8,128)(2,1)S(1)}, u32[]{:S(2)}, u32[]{:S(2)}) collective-permute-start(bf16[16,8192]{1,0:T(8,128)(2,1)} %refs_0_.1), channel_id=1, source_target_pairs={{0,6},{1,7},{2,4},{3,5},{4,2},{5,3},{6,0},{7,1},{8,14},{9,15},{10,... | collective-permute-start | bytes 786440 | tf_op jit(solution)/shard_map/ppermute | solution.py:374
  23.2 24.8 %collective-permute-start.6 = (bf16[16,8192]{1,0:T(8,128)(2,1)}, bf16[16,8192]{1,0:T(8,128)(2,1)S(1)}, u32[]{:S(2)}, u32[]{:S(2)}) collective-permute-start(bf16[16,8192]{1,0:T(8,128)(2,1)} %refs_0_.1), channel_id=1, source_target_pairs={{0,7},{1,6},{2,5},{3,4},{4,3},{5,2},{6,1},{7,0},{8,15},{9,14},{10,... | collective-permute-start | bytes 786440 | tf_op jit(solution)/shard_map/ppermute | solution.py:374
  23.2 24.8 %copy-start = (bf16[8192,256]{1,0:T(8,128)(2,1)S(1)}, bf16[8192,256]{1,0:T(8,128)(2,1)}, u32[]{:S(2)}) copy-start(bf16[8192,256]{1,0:T(8,128)(2,1)} %refs_8_.1) | copy-start | bytes 12582916
  23.2 24.8 %copy-start.1 = (bf16[1,30,64,256]{3,2,1,0:T(8,128)(2,1)S(1)}, bf16[1,30,64,256]{3,2,1,0:T(8,128)(2,1)}, u32[]{:S(2)}) copy-start(bf16[1,30,64,256]{3,2,1,0:T(8,128)(2,1)} %param.11) | copy-start | bytes 2949124
  23.2 24.8 %copy-start.2 = (bf16[16,8192]{1,0:T(8,128)(2,1)S(1)}, bf16[16,8192]{1,0:T(8,128)(2,1)}, u32[]{:S(2)}) copy-start(bf16[16,8192]{1,0:T(8,128)(2,1)} %refs_0_.1) | copy-start | bytes 786436
  23.2 24.8 %copy-start.3 = (s32[16,128]{1,0:T(8,128)S(1)}, s32[16,128]{1,0:T(8,128)}, u32[]{:S(2)}) copy-start(s32[16,128]{1,0:T(8,128)} %get-tuple-element.13.pick_ref) | copy-start | bytes 24580
  23.2 24.8 %copy-start.4 = (bf16[256]{0:T(256)(128)(2,1)S(1)}, bf16[256]{0:T(256)(128)(2,1)}, u32[]{:S(2)}) copy-start(bf16[256]{0:T(256)(128)(2,1)} %refs_9_.1) | copy-start | bytes 1540
  51.5 25.3 %all-to-all-start = ((bf16[16,2,64,256]{3,2,1,0:T(8,128)(2,1)}), bf16[16,2,64,256]{3,2,1,0:T(8,128)(2,1)S(1)}, u32[]{:S(2)}, u32[]{:S(2)}) async-start(bf16[16,2,64,256]{3,2,1,0:T(8,128)(2,1)} %fresh.1), calls=%async_computation | async-start | bytes 2097152 | tf_op jit(solution)/shard_map/all_to_all | solution.py:402

commit v4 on v3

--- a/solution.py
+++ b/solution.py
@@ -58,9 +58,11 @@
     ]
 
 
-def route_kernel(groups, parent_ref, child_ref, len_ref, cached_ref, pick_ref, bias_a_ref, bias_b_ref, send_ref, pick_v, pick_s, sem):
+def route_kernel(groups, parent_ref, child_ref, len_ref, cached_ref, pick_ref, bias_a_ref, bias_b_ref, send_ref, pick_v, pick_s, cached_v, sem):
     me = lax.axis_index("group")
     cached_nodes = cached_ref.shape[0]
+    fetch = pltpu.make_async_copy(cached_ref, cached_v, sem.at[1])
+    fetch.start()
     per_node = cached_nodes + FRESH
     width = 128
     parent = parent_ref[...]
@@ -76,8 +78,9 @@
         tables = rows_of(jump)
         ahead = jnp.where(path < none, lookup(tables, jnp.minimum(path, none - 1)), none)
         path = jnp.where((lane >= reach) & (lane < 2 * reach), pltpu.roll(ahead, reach, 1), path)
-        jump = jnp.where(jump < none, lookup(tables, jnp.minimum(jump, none - 1)), none)
         reach *= 2
+        if reach < 64:
+            jump = jnp.where(jump < none, lookup(tables, jnp.minimum(jump, none - 1)), none)
     inner = path % per_node
     there = path < none
     picks = slot_sums(
@@ -89,7 +92,7 @@
     pick = pick.astype(jnp.int32)
     pick_v[...] = pick
     pick_ref[...] = pick
-    copy = pltpu.make_async_copy(pick_v, pick_s, sem)
+    copy = pltpu.make_async_copy(pick_v, pick_s, sem.at[0])
     copy.start()
     mine = jnp.sum(jnp.where(group_row == me, path, 0).astype(jnp.float32), axis=0, keepdims=True)
     mine = jnp.broadcast_to(mine, (groups, width)).astype(jnp.int32)
@@ -104,10 +107,11 @@
         limit = jnp.where(lane < half, valid[first], valid[first + 1])
         ref[...] = jnp.where(token < limit, 0.0, LOW)
     copy.wait()
+    fetch.wait()
     for g in range(groups):
         for s in range(2):
             node = jnp.minimum(pick_s[g, s], cached_nodes - 1)
-            send_ref[g, s] = cached_ref[node]
+            send_ref[g, s] = cached_v[node]
 
 
 def route(parent, child_parent, node_len, cached):
@@ -121,7 +125,7 @@
         parent.reshape(rows, 128),
         child_parent,
         node_len.reshape(rows, 128),
-        cached,
+        pltpu.with_memory_space_constraint(cached, pltpu.HBM),
     )
     return pl.pallas_call(
         functools.partial(route_kernel, groups),
@@ -130,13 +134,14 @@
             spec(args[0].shape),
             pl.BlockSpec(memory_space=pltpu.SMEM),
             spec(args[2].shape),
-            spec(args[3].shape),
+            pl.BlockSpec(memory_space=pl.ANY),
         ],
         out_specs=[spec(o.shape) for o in out],
         scratch_shapes=[
             pltpu.VMEM((groups, 128), jnp.int32),
             pltpu.SMEM((groups, 128), jnp.int32),
-            pltpu.SemaphoreType.DMA,
+            pltpu.VMEM(cached.shape, cached.dtype),
+            pltpu.SemaphoreType.DMA((2,)),
         ],
         cost_estimate=pl.CostEstimate(flops=2**24, bytes_accessed=2**21, transcendentals=0),
         name="route",
@@ -145,30 +150,21 @@
 
 def fresh_kernel(parts, pick_ref, *refs):
     hidden_refs = refs[:parts]
-    weight_ref, bias_ref, cached_ref, send_ref, total, table, hidden = refs[parts:]
-    step = pl.program_id(0)
+    weight_ref, bias_ref, cached_ref, send_ref, table, hidden = refs[parts:]
+    cached_nodes, tokens, _ = cached_ref.shape
     me = lax.axis_index("tp")
-    cached_nodes, tokens, _ = cached_ref.shape
-
-    @pl.when(step == 0)
-    def _():
-        total[...] = jnp.zeros_like(total)
-        table[:cached_nodes] = cached_ref[...]
-
     for k, ref in enumerate(hidden_refs):
         block = ref.shape[0]
         hidden[pl.ds(pl.multiple_of((me ^ k) * block, block), block), :] = ref[...]
-    total[...] += jnp.dot(hidden[...], weight_ref[...], preferred_element_type=jnp.float32)
-
-    @pl.when(step == pl.num_programs(0) - 1)
-    def _():
-        rows = (total[...] + bias_ref[...].astype(jnp.float32)[None, :]).astype(jnp.bfloat16)
-        for f in range(FRESH):
-            table[cached_nodes + f] = rows[f * tokens : (f + 1) * tokens]
-        for g in range(send_ref.shape[0]):
-            for s in range(2):
-                node = jnp.clip(pick_ref[g, 2 + s], 0, cached_nodes + FRESH - 1)
-                send_ref[g, s] = table[node]
+    table[:cached_nodes] = cached_ref[...]
+    total = jnp.dot(hidden[...], weight_ref[...], preferred_element_type=jnp.float32)
+    rows = (total + bias_ref[...].astype(jnp.float32)[None, :]).astype(jnp.bfloat16)
+    for f in range(FRESH):
+        table[cached_nodes + f] = rows[f * tokens : (f + 1) * tokens]
+    for g in range(send_ref.shape[0]):
+        for s in range(2):
+            node = jnp.clip(pick_ref[g, 2 + s], 0, cached_nodes + FRESH - 1)
+            send_ref[g, s] = table[node]
 
 
 def project_fresh(pick, hidden, weight, bias, cached):
@@ -176,23 +172,15 @@
     nodes, tokens, width = cached.shape
     block, depth = hidden[0].shape
     rows = block * len(hidden)
-    step = 2048
+    on_chip = pl.BlockSpec(memory_space=pltpu.VMEM)
     return pl.pallas_call(
         functools.partial(fresh_kernel, len(hidden)),
-        grid=(depth // step,),
         out_shape=jax.ShapeDtypeStruct((groups, 2, tokens, width), cached.dtype),
-        in_specs=[
-            pl.BlockSpec(memory_space=pltpu.SMEM),
-            *[pl.BlockSpec((block, step), lambda i: (0, i)) for _ in hidden],
-            pl.BlockSpec((step, width), lambda i: (i, 0)),
-            spec((width,)),
-            spec(cached.shape),
-        ],
+        in_specs=[pl.BlockSpec(memory_space=pltpu.SMEM)] + [on_chip] * (len(hidden) + 3),
         out_specs=spec((groups, 2, tokens, width)),
         scratch_shapes=[
-            pltpu.VMEM((rows, width), jnp.float32),
             pltpu.VMEM((nodes + FRESH, tokens, width), cached.dtype),
-            pltpu.VMEM((rows, step), cached.dtype),
+            pltpu.VMEM((rows, depth), cached.dtype),
         ],
         compiler_params=pltpu.CompilerParams(vmem_limit_bytes=SMALL_LIMIT),
         cost_estimate=pl.CostEstimate(
@@ -295,14 +283,29 @@
     total[:, head:] = jnp.broadcast_to(stat_ref[:, head - 1 :], (rows, head))
 
 
+def merge_state(stat_ref, acc_ref, maximum, total):
+    rows, head = acc_ref.shape
+    old = jnp.broadcast_to(stat_ref[:, :1], (rows, head))
+    summed = jnp.broadcast_to(stat_ref[:, head - 1 :], (rows, head))
+    new = jnp.maximum(old, maximum[...])
+    theirs, ours = jnp.exp2(old - new), jnp.exp2(maximum[...] - new)
+    maximum[...] = new
+    total[:, :head] = total[:, :head] * ours + acc_ref[...] * theirs
+    total[:, head:] = total[:, head:] * ours + summed * theirs
+
+
+def empty_state(maximum, total):
+    maximum[...] = jnp.full_like(maximum, LOW)
+    total[...] = jnp.zeros_like(total)
+
+
 def first_kernel(scale, q_ref, prefix_ref, stat_ref, acc_ref, query, maximum, total):
     step = pl.program_id(0)
 
     @pl.when(step == 0)
     def _():
         load_query(q_ref, query)
-        maximum[...] = jnp.full_like(maximum, LOW)
-        total[...] = jnp.zeros_like(total)
+        empty_state(maximum, total)
 
     take_keys(query, maximum, total, plain_pieces(prefix_ref), scale)
 
@@ -311,13 +314,17 @@
         put_state(maximum, total, stat_ref, acc_ref)
 
 
-def middle_kernel(scale, steps, blocks, q_ref, prefix_ref, path_ref, bias_ref, own_ref, stat_in, acc_in, stat_ref, acc_ref, query, maximum, total):
+def middle_kernel(scale, steps, blocks, q_ref, prefix_ref, path_ref, bias_ref, own_ref, stat_in, acc_in, stat_ref, acc_ref, query, maximum, total, stat_v, acc_v, path_v, sem):
     step = pl.program_id(0)
+    pairs = ((path_ref, path_v), (stat_in, stat_v), (acc_in, acc_v))
+    copies = [pltpu.make_async_copy(a, b, sem.at[k]) for k, (a, b) in enumerate(pairs)]
 
     @pl.when(step == 0)
     def _():
+        for copy in copies:
+            copy.start()
         load_query(q_ref, query)
-        get_state(stat_in, acc_in, maximum, total)
+        empty_state(maximum, total)
 
     @pl.when(step < blocks)
     def _():
@@ -325,8 +332,11 @@
 
     @pl.when(step == blocks)
     def _():
-        pieces = masked_pieces(path_ref, bias_ref) + own_piece(own_ref, steps)
+        for copy in copies:
+            copy.wait()
+        pieces = masked_pieces(path_v, bias_ref) + own_piece(own_ref, steps)
         take_keys(query, maximum, total, pieces, scale)
+        merge_state(stat_v, acc_v, maximum, total)
         put_state(maximum, total, stat_ref, acc_ref)
 
 
@@ -370,9 +380,15 @@
     queries = rows * (decode_q.shape[1] // head)
     tp = lax.axis_size("tp")
 
-    hidden = [fresh_hidden] + [
-        lax.ppermute(fresh_hidden, "tp", [(t, t ^ k) for t in range(tp)]) for k in range(1, tp)
-    ]
+    def moved(block, distance):
+        return lax.ppermute(block, "tp", [(t, t ^ distance) for t in range(tp)])
+
+    hidden = [fresh_hidden] * tp
+    for k in (1, 2, 4, 5):
+        hidden[k] = moved(fresh_hidden, k)
+    hidden[6] = moved(fresh_hidden, 6)
+    hidden[7] = moved(hidden[1], 6)
+    hidden[3] = moved(hidden[1], 2)
     pick, bias_a, bias_b, send_a = route(parent, child_parent, node_len, cached)
     path_a = lax.all_to_all(send_a, "group", 0, 0, tiled=True).reshape(-1, 2 * head)
 
@@ -386,6 +402,8 @@
     prefix = pltpu.with_memory_space_constraint(prefix, pltpu.HBM)
     all_blocks = prefix.shape[0] // BLOCK
     blocks = all_blocks - FIRST_BLOCKS
+    anywhere = pl.BlockSpec(memory_space=pl.ANY)
+    state_scratch = [pltpu.VMEM(s.shape, s.dtype) for s in state]
     stat, acc = pl.pallas_call(
         functools.partial(first_kernel, scale),
         grid=(FIRST_BLOCKS,),
@@ -400,7 +418,9 @@
 
     send_b = project_fresh(pick, hidden, key_value_weight, key_value_bias, cached)
     path_b = lax.all_to_all(send_b, "group", 0, 0, tiled=True).reshape(-1, 2 * head)
+    path_a = pltpu.with_memory_space_constraint(path_a, pltpu.HBM)
     path_b = pltpu.with_memory_space_constraint(path_b, pltpu.VMEM)
+    stat, acc = (pltpu.with_memory_space_constraint(a, pltpu.HBM) for a in (stat, acc))
 
     stat, acc = pl.pallas_call(
         functools.partial(middle_kernel, scale, steps, blocks),
@@ -411,14 +431,16 @@
             pl.BlockSpec(
                 (BLOCK, 2 * head), lambda i: (jnp.minimum(i + FIRST_BLOCKS, all_blocks - 1), 0)
             ),
-            spec(path_a.shape),
+            anywhere,
             spec(bias_a.shape),
             spec(own.shape),
-            spec(state[0].shape),
-            spec(state[1].shape),
+            anywhere,
+            anywhere,
         ],
         out_specs=[spec(s.shape) for s in state],
-        scratch_shapes=scratch,
+        scratch_shapes=scratch
+        + state_scratch
+        + [pltpu.VMEM(path_a.shape, path_a.dtype), pltpu.SemaphoreType.DMA((3,))],
         compiler_params=params,
         cost_estimate=attention_cost(queries, head, blocks * BLOCK + path_a.shape[0]),
         name="attend_middle",

time: 81.9 us -> 74.5 us (0.910)
  waiting for transfers between devices: 11.5 us -> 8.13 us
  Pallas kernels: 42.9 us -> 40.9 us
  starting transfers between devices: 27.1 us -> 25.1 us
    ppermute x7, waiting for transfers between devices: 11.5 us -> 7.68 us  [moved(): return lax.ppermute(block, 'tp', [(t, t ^ distance) for t in range(tp)])]
    ppermute x7, starting transfers between devices: 11.1 us -> 9.89 us  [moved(): return lax.ppermute(block, 'tp', [(t, t ^ distance) for t in range(tp)])]
    pallas_call x1, Pallas kernels: 3.49 us -> 2.57 us  [project_fresh(): pl.pallas_call(functools.partial(fresh_kernel, len(hidden)), out_shape=ja...]
  transfers between devices with their start and end apart: 9 -> 9, of which waited for: 2 -> 4; matrix products, arithmetic and copies ran while one was open for 0% -> 0% of each run, Pallas kernels for 47% -> 49%
where the time goes in v4:
time: 74.5 us; the launch traced here: 74.2 us
  Pallas kernels  40.9 us (55%)
  starting transfers between devices  25.1 us (34%)
  waiting for transfers between devices  8.13 us (11%)
    pallas_call x1, Pallas kernels, per_device(): pl.pallas_call(functools.partial(middle_kernel, scale, steps, blocks), gr...  16.6 us
    pallas_call x1, Pallas kernels, per_device(): pl.pallas_call(functools.partial(first_kernel, scale), grid=(FIRST_BLOCKS...  13.2 us
    ppermute x7, starting transfers between devices, moved(): return lax.ppermute(block, 'tp', [(t, t ^ distance) for t in range(tp)])  9.89 us
    all_to_all x1, starting transfers between devices, per_device(): lax.all_to_all(send_a, 'group', 0, 0, tiled=True).reshape(-1, 2 * head)  7.9 us
    ppermute x7, waiting for transfers between devices, moved(): return lax.ppermute(block, 'tp', [(t, t ^ distance) for t in range(tp)])  7.68 us
    all_to_all x1, starting transfers between devices, per_device(): lax.all_to_all(send_b, 'group', 0, 0, tiled=True).reshape(-1, 2 * head)  7.32 us
    pallas_call x1, Pallas kernels, per_device(): pl.pallas_call(functools.partial(last_kernel, scale), out_shape=jax.Shape...  4.8 us
    pallas_call x1, Pallas kernels, route(): pl.pallas_call(functools.partial(route_kernel, groups), out_shape=out, in...  3.69 us
  transfers between devices with their start and end apart: 9, of which 4 were waited for; matrix products, arithmetic and copies ran while one was open for 0% of the time, Pallas kernels for 49%

profile of v4, /device:TPU:1, one launch (start us, length us, event | category | flops | bytes accessed | tf_op | source)
XLA Modules:
  0.0 74.2 jit_solution(8096561279086550481)
XLA Ops:
  0.0 2.0 %collective-permute-start = (bf16[16,8192]{1,0:T(8,128)(2,1)}, bf16[16,8192]{1,0:T(8,128)(2,1)S(1)}, u32[]{:S(2)}, u32[]{:S(2)}) collective-permute-start(bf16[16,8192]{1,0:T(8,128)(2,1)} %refs_0_.1), channel_id=1, source_target_pairs={{0,1},{1,0},{2,3},{3,2},{4,5},{5,4},{6,7},{7,6},{8,9},{9,8},{10,11... | collective-permute-start | bytes 786440 | tf_op jit(solution)/shard_map/ppermute | solution.py:384
  2.0 1.6 %collective-permute-start.1 = (bf16[16,8192]{1,0:T(8,128)(2,1)}, bf16[16,8192]{1,0:T(8,128)(2,1)S(1)}, u32[]{:S(2)}, u32[]{:S(2)}) collective-permute-start(bf16[16,8192]{1,0:T(8,128)(2,1)} %refs_0_.1), channel_id=1, source_target_pairs={{0,2},{1,3},{2,0},{3,1},{4,6},{5,7},{6,4},{7,5},{8,10},{9,11},{10,... | collective-permute-start | bytes 786440 | tf_op jit(solution)/shard_map/ppermute | solution.py:384
  3.7 3.7 %route.1 = (s32[16,128]{1,0:T(8,128)}, f32[16,128]{1,0:T(8,128)}, f32[16,128]{1,0:T(8,128)}, bf16[16,2,64,256]{3,2,1,0:T(8,128)(2,1)}) custom-call(s32[4,128]{1,0:T(4,128)} %bitcast.10, s32[16]{0:T(128)} %child_ref.1, s32[4,128]{1,0:T(4,128)} %bitcast.11, bf16[30,64,256]{2,1,0:T(8,128)(2,1)} %bitcast.7), custom_call_target="tpu_custom_call" | custom-call | flops 16777216 | bytes 2097152 | tf_op jit(solution)/shard_map/route/pallas_call | solution.py:130
  7.4 7.9 %all-to-all-start.1 = ((bf16[16,2,64,256]{3,2,1,0:T(8,128)(2,1)}), bf16[16,2,64,256]{3,2,1,0:T(8,128)(2,1)}, u32[]{:S(2)}, u32[]{:S(2)}) async-start(bf16[16,2,64,256]{3,2,1,0:T(8,128)(2,1)} %get-tuple-element.15), calls=%async_computation.1 | async-start | bytes 2097152 | tf_op jit(solution)/shard_map/all_to_all | solution.py:393
  15.3 3.3 %collective-permute-start.3 = (bf16[16,8192]{1,0:T(8,128)(2,1)}, bf16[16,8192]{1,0:T(8,128)(2,1)S(1)}, u32[]{:S(2)}, u32[]{:S(2)}) collective-permute-start(bf16[16,8192]{1,0:T(8,128)(2,1)} %refs_0_.1), channel_id=1, source_target_pairs={{0,4},{1,5},{2,6},{3,7},{4,0},{5,1},{6,2},{7,3},{8,12},{9,13},{10,... | collective-permute-start | bytes 786440 | tf_op jit(solution)/shard_map/ppermute | solution.py:384
  18.6 0.0 collective-permute-start.4
  18.6 1.6 %collective-permute-start.5 = (bf16[16,8192]{1,0:T(8,128)(2,1)}, bf16[16,8192]{1,0:T(8,128)(2,1)S(1)}, u32[]{:S(2)}, u32[]{:S(2)}) collective-permute-start(bf16[16,8192]{1,0:T(8,128)(2,1)} %refs_0_.1), channel_id=1, source_target_pairs={{0,6},{1,7},{2,4},{3,5},{4,2},{5,3},{6,0},{7,1},{8,14},{9,15},{10,... | collective-permute-start | bytes 786440 | tf_op jit(solution)/shard_map/ppermute | solution.py:384
  20.1 0.0 collective-permute-done.refs_1_
  20.1 0.7 collective-permute-start.2
  20.9 0.0 collective-permute-done.1.refs_2_
  20.9 0.6 collective-permute-start.6
  21.5 0.0 copy-start
  21.5 0.0 copy-start.1
  21.5 0.0 copy-start.2
  21.5 0.0 copy-start.4
  21.5 13.2 %attend_first.1 = (f32[1024,128]{1,0:T(8,128)}, f32[1024,128]{1,0:T(8,128)}) custom-call(bf16[128,1024]{1,0:T(8,128)(2,1)} %q_ref.5, bf16[16384,256]{1,0:T(8,128)(2,1)} %bitcast.12), custom_call_target="tpu_custom_call" | custom-call | flops 8589934592 | bytes 4194304 | tf_op jit(solution)/shard_map/attend_first/pallas_call | solution.py:407
  34.7 0.0 collective-permute-done.3.refs_4_
  34.7 1.7 %collective-permute-done.4.refs_5_ = bf16[16,8192]{1,0:T(8,128)(2,1)S(1)} collective-permute-done((bf16[16,8192]{1,0:T(8,128)(2,1)}, bf16[16,8192]{1,0:T(8,128)(2,1)S(1)}, u32[]{:S(2)}, u32[]{:S(2)}) %collective-permute-start.4) | collective-permute-done | bytes 262176 | tf_op jit(solution)/shard_map/ppermute | solution.py:384
  36.4 0.4 collective-permute-done.5.refs_6_
  36.8 0.0 collective-permute-done.2.refs_3_
  36.8 5.6 %collective-permute-done.6.refs_7_ = bf16[16,8192]{1,0:T(8,128)(2,1)S(1)} collective-permute-done((bf16[16,8192]{1,0:T(8,128)(2,1)S(1)}, bf16[16,8192]{1,0:T(8,128)(2,1)S(1)}, u32[]{:S(2)}, u32[]{:S(2)}) %collective-permute-start.6) | collective-permute-done | bytes 262176 | tf_op jit(solution)/shard_map/ppermute | solution.py:384
  42.4 0.0 copy-done
  42.4 0.0 copy-done.1
  42.4 0.0 copy-done.2
  42.4 0.0 copy-done.3
  42.4 0.0 copy-done.4
  42.4 2.6 %fresh.1 = bf16[16,2,64,256]{3,2,1,0:T(8,128)(2,1)} custom-call(s32[16,128]{1,0:T(8,128)S(1)} %copy-done.3, bf16[16,8192]{1,0:T(8,128)(2,1)S(1)} %copy-done.2, bf16[16,8192]{1,0:T(8,128)(2,1)S(1)} %collective-permute-done.refs_1_, bf16[16,8192]{1,0:T(8,128)(2,1)S(1)} %collective-permute-done.1.refs_2_, bf16[16,8192]{1,0:T(8,128)(2,1)S(1)} %collective-permute-done.2.refs_3_, ...), custom_call_target="tpu_custom_call" | custom-call | flops 536870912 | bytes 8388608 | tf_op jit(solution)/shard_map/fresh/pallas_call | solution.py:176
  45.0 0.0 all-to-all-done.1
  45.0 7.3 %all-to-all-start = ((bf16[16,2,64,256]{3,2,1,0:T(8,128)(2,1)}), bf16[16,2,64,256]{3,2,1,0:T(8,128)(2,1)S(1)}, u32[]{:S(2)}, u32[]{:S(2)}) async-start(bf16[16,2,64,256]{3,2,1,0:T(8,128)(2,1)} %fresh.1), calls=%async_computation | async-start | bytes 2097152 | tf_op jit(solution)/shard_map/all_to_all | solution.py:420
  52.3 16.6 %attend_middle.1 = (f32[1024,128]{1,0:T(8,128)}, f32[1024,128]{1,0:T(8,128)}) custom-call(bf16[128,1024]{1,0:T(8,128)(2,1)} %q_ref.5, bf16[16384,256]{1,0:T(8,128)(2,1)} %bitcast.13, bf16[2048,256]{1,0:T(8,128)(2,1)} %bitcast.5.path_ref, f32[16,128]{1,0:T(8,128)} %get-tuple-element.16.bias_ref, bf16[128,256]{1,0:T(8,128)(2,1)} %bitcast.14, ...), custom_call_target="tpu_custom_call" | custom-call | flops 10737418240 | bytes 5242880 | tf_op jit(solution)/shard_map/attend_middle/pallas_call | solution.py:425
  69.0 0.4 all-to-all-done
  69.4 4.8 %attend_last.1 = bf16[128,1024]{1,0:T(8,128)(2,1)} custom-call(bf16[128,1024]{1,0:T(8,128)(2,1)} %q_ref.5, bf16[2048,256]{1,0:T(8,128)(2,1)S(1)} %bitcast.9, f32[16,128]{1,0:T(8,128)} %get-tuple-element.14.bias_ref, f32[1024,128]{1,0:T(8,128)} %get-tuple-element.19.stat_in, f32[1024,128]{1,0:T(8,128)} %get-tuple-element.20.acc_in), custom_call_target="tpu_custom_call" | custom-call | flops 2147483648 | bytes 1048576 | tf_op jit(solution)/shard_map/attend_last/pallas_call | solution.py:449
  (1 shorter events, 0.0 us)
Async XLA Ops:
  0.0 20.1 %collective-permute-start = (bf16[16,8192]{1,0:T(8,128)(2,1)}, bf16[16,8192]{1,0:T(8,128)(2,1)S(1)}, u32[]{:S(2)}, u32[]{:S(2)}) collective-permute-start(bf16[16,8192]{1,0:T(8,128)(2,1)} %refs_0_.1), channel_id=1, source_target_pairs={{0,1},{1,0},{2,3},{3,2},{4,5},{5,4},{6,7},{7,6},{8,9},{9,8},{10,11... | collective-permute-start | bytes 786440 | tf_op jit(solution)/shard_map/ppermute | solution.py:384
  2.0 18.9 %collective-permute-start.1 = (bf16[16,8192]{1,0:T(8,128)(2,1)}, bf16[16,8192]{1,0:T(8,128)(2,1)S(1)}, u32[]{:S(2)}, u32[]{:S(2)}) collective-permute-start(bf16[16,8192]{1,0:T(8,128)(2,1)} %refs_0_.1), channel_id=1, source_target_pairs={{0,2},{1,3},{2,0},{3,1},{4,6},{5,7},{6,4},{7,5},{8,10},{9,11},{10,... | collective-permute-start | bytes 786440 | tf_op jit(solution)/shard_map/ppermute | solution.py:384
  7.4 37.6 %all-to-all-start.1 = ((bf16[16,2,64,256]{3,2,1,0:T(8,128)(2,1)}), bf16[16,2,64,256]{3,2,1,0:T(8,128)(2,1)}, u32[]{:S(2)}, u32[]{:S(2)}) async-start(bf16[16,2,64,256]{3,2,1,0:T(8,128)(2,1)} %get-tuple-element.15), calls=%async_computation.1 | async-start | bytes 2097152 | tf_op jit(solution)/shard_map/all_to_all | solution.py:393
  15.3 19.5 %collective-permute-start.3 = (bf16[16,8192]{1,0:T(8,128)(2,1)}, bf16[16,8192]{1,0:T(8,128)(2,1)S(1)}, u32[]{:S(2)}, u32[]{:S(2)}) collective-permute-start(bf16[16,8192]{1,0:T(8,128)(2,1)} %refs_0_.1), channel_id=1, source_target_pairs={{0,4},{1,5},{2,6},{3,7},{4,0},{5,1},{6,2},{7,3},{8,12},{9,13},{10,... | collective-permute-start | bytes 786440 | tf_op jit(solution)/shard_map/ppermute | solution.py:384
  18.6 17.8 %collective-permute-start.4 = (bf16[16,8192]{1,0:T(8,128)(2,1)}, bf16[16,8192]{1,0:T(8,128)(2,1)S(1)}, u32[]{:S(2)}, u32[]{:S(2)}) collective-permute-start(bf16[16,8192]{1,0:T(8,128)(2,1)} %refs_0_.1), channel_id=1, source_target_pairs={{0,5},{1,4},{2,7},{3,6},{4,1},{5,0},{6,3},{7,2},{8,13},{9,12},{10,... | collective-permute-start | bytes 786440 | tf_op jit(solution)/shard_map/ppermute | solution.py:384
  18.6 18.2 %collective-permute-start.5 = (bf16[16,8192]{1,0:T(8,128)(2,1)}, bf16[16,8192]{1,0:T(8,128)(2,1)S(1)}, u32[]{:S(2)}, u32[]{:S(2)}) collective-permute-start(bf16[16,8192]{1,0:T(8,128)(2,1)} %refs_0_.1), channel_id=1, source_target_pairs={{0,6},{1,7},{2,4},{3,5},{4,2},{5,3},{6,0},{7,1},{8,14},{9,15},{10,... | collective-permute-start | bytes 786440 | tf_op jit(solution)/shard_map/ppermute | solution.py:384
  20.1 16.6 %collective-permute-start.2 = (bf16[16,8192]{1,0:T(8,128)(2,1)S(1)}, bf16[16,8192]{1,0:T(8,128)(2,1)S(1)}, u32[]{:S(2)}, u32[]{:S(2)}) collective-permute-start(bf16[16,8192]{1,0:T(8,128)(2,1)S(1)} %collective-permute-done.refs_1_), channel_id=1, source_target_pairs={{0,2},{1,3},{2,0},{3,1},{4,6},{5,7},{6,4},{7,5},{8,10},{9,11},{10,... | collective-permute-start | bytes 786440 | tf_op jit(solution)/shard_map/ppermute | solution.py:384
  20.9 21.5 %collective-permute-start.6 = (bf16[16,8192]{1,0:T(8,128)(2,1)S(1)}, bf16[16,8192]{1,0:T(8,128)(2,1)S(1)}, u32[]{:S(2)}, u32[]{:S(2)}) collective-permute-start(bf16[16,8192]{1,0:T(8,128)(2,1)S(1)} %collective-permute-done.refs_1_), channel_id=1, source_target_pairs={{0,6},{1,7},{2,4},{3,5},{4,2},{5,3},{6,0},{7,1},{8,14},{9,15},{10,... | collective-permute-start | bytes 786440 | tf_op jit(solution)/shard_map/ppermute | solution.py:384
  21.5 20.9 %copy-start = (bf16[8192,256]{1,0:T(8,128)(2,1)S(1)}, bf16[8192,256]{1,0:T(8,128)(2,1)}, u32[]{:S(2)}) copy-start(bf16[8192,256]{1,0:T(8,128)(2,1)} %refs_8_.1) | copy-start | bytes 12582916
  21.5 20.9 %copy-start.1 = (bf16[1,30,64,256]{3,2,1,0:T(8,128)(2,1)S(1)}, bf16[1,30,64,256]{3,2,1,0:T(8,128)(2,1)}, u32[]{:S(2)}) copy-start(bf16[1,30,64,256]{3,2,1,0:T(8,128)(2,1)} %param.11) | copy-start | bytes 2949124
  21.5 20.9 %copy-start.2 = (bf16[16,8192]{1,0:T(8,128)(2,1)S(1)}, bf16[16,8192]{1,0:T(8,128)(2,1)}, u32[]{:S(2)}) copy-start(bf16[16,8192]{1,0:T(8,128)(2,1)} %refs_0_.1) | copy-start | bytes 786436
  21.5 20.9 %copy-start.3 = (s32[16,128]{1,0:T(8,128)S(1)}, s32[16,128]{1,0:T(8,128)}, u32[]{:S(2)}) copy-start(s32[16,128]{1,0:T(8,128)} %get-tuple-element.13.pick_ref) | copy-start | bytes 24580
  21.5 20.9 %copy-start.4 = (bf16[256]{0:T(256)(128)(2,1)S(1)}, bf16[256]{0:T(256)(128)(2,1)}, u32[]{:S(2)}) copy-start(bf16[256]{0:T(256)(128)(2,1)} %refs_9_.1) | copy-start | bytes 1540
  45.0 24.4 %all-to-all-start = ((bf16[16,2,64,256]{3,2,1,0:T(8,128)(2,1)}), bf16[16,2,64,256]{3,2,1,0:T(8,128)(2,1)S(1)}, u32[]{:S(2)}, u32[]{:S(2)}) async-start(bf16[16,2,64,256]{3,2,1,0:T(8,128)(2,1)} %fresh.1), calls=%async_computation | async-start | bytes 2097152 | tf_op jit(solution)/shard_map/all_to_all | solution.py:420

commit v5 on v4

--- a/solution.py
+++ b/solution.py
@@ -11,8 +11,9 @@
 FRESH = 2
 SUB = 512
 ROWS = 256
-BLOCK = 4096
-FIRST_BLOCKS = 2
+PART = 2048
+FIRST_PARTS = 3
+MIDDLE_STEPS = 2
 LOW = -1e30
 LOG2E = 1.4426950408889634
 VMEM_LIMIT = 56 * 2**20
@@ -276,13 +277,6 @@
     acc_ref[...] = total[:, :head]
 
 
-def get_state(stat_ref, acc_ref, maximum, total):
-    rows, head = acc_ref.shape
-    maximum[...] = jnp.broadcast_to(stat_ref[:, :1], (rows, head))
-    total[:, :head] = acc_ref[...]
-    total[:, head:] = jnp.broadcast_to(stat_ref[:, head - 1 :], (rows, head))
-
-
 def merge_state(stat_ref, acc_ref, maximum, total):
     rows, head = acc_ref.shape
     old = jnp.broadcast_to(stat_ref[:, :1], (rows, head))
@@ -299,22 +293,16 @@
     total[...] = jnp.zeros_like(total)
 
 
-def first_kernel(scale, q_ref, prefix_ref, stat_ref, acc_ref, query, maximum, total):
-    step = pl.program_id(0)
-
-    @pl.when(step == 0)
-    def _():
-        load_query(q_ref, query)
-        empty_state(maximum, total)
-
-    take_keys(query, maximum, total, plain_pieces(prefix_ref), scale)
-
-    @pl.when(step == pl.num_programs(0) - 1)
-    def _():
-        put_state(maximum, total, stat_ref, acc_ref)
-
-
-def middle_kernel(scale, steps, blocks, q_ref, prefix_ref, path_ref, bias_ref, own_ref, stat_in, acc_in, stat_ref, acc_ref, query, maximum, total, stat_v, acc_v, path_v, sem):
+def first_kernel(scale, q_ref, *refs):
+    prefix_refs, (stat_ref, acc_ref, query, maximum, total) = refs[:FIRST_PARTS], refs[FIRST_PARTS:]
+    load_query(q_ref, query)
+    empty_state(maximum, total)
+    pieces = [piece for ref in prefix_refs for piece in plain_pieces(ref)]
+    take_keys(query, maximum, total, pieces, scale)
+    put_state(maximum, total, stat_ref, acc_ref)
+
+
+def middle_kernel(scale, steps, blocks, q_ref, prefix_ref, path_ref, bias_ref, own_ref, stat_in, acc_in, maximum, total, query, stat_v, acc_v, path_v, sem):
     step = pl.program_id(0)
     pairs = ((path_ref, path_v), (stat_in, stat_v), (acc_in, acc_v))
     copies = [pltpu.make_async_copy(a, b, sem.at[k]) for k, (a, b) in enumerate(pairs)]
@@ -337,12 +325,12 @@
         pieces = masked_pieces(path_v, bias_ref) + own_piece(own_ref, steps)
         take_keys(query, maximum, total, pieces, scale)
         merge_state(stat_v, acc_v, maximum, total)
-        put_state(maximum, total, stat_ref, acc_ref)
-
-
-def last_kernel(scale, q_ref, path_ref, bias_ref, stat_in, acc_in, out_ref, query, maximum, total):
+
+
+def last_kernel(scale, q_ref, path_ref, bias_ref, max_in, total_in, out_ref, query, maximum, total):
     load_query(q_ref, query)
-    get_state(stat_in, acc_in, maximum, total)
+    maximum[...] = max_in[...]
+    total[...] = total_in[...]
     take_keys(query, maximum, total, masked_pieces(path_ref, bias_ref), scale)
     rows, head = q_ref.shape[0], query.shape[1]
     for j in range(q_ref.shape[1] // head):
@@ -384,10 +372,10 @@
         return lax.ppermute(block, "tp", [(t, t ^ distance) for t in range(tp)])
 
     hidden = [fresh_hidden] * tp
-    for k in (1, 2, 4, 5):
+    for k in (1, 2, 6, 5):
         hidden[k] = moved(fresh_hidden, k)
-    hidden[6] = moved(fresh_hidden, 6)
     hidden[7] = moved(hidden[1], 6)
+    hidden[4] = moved(hidden[6], 2)
     hidden[3] = moved(hidden[1], 2)
     pick, bias_a, bias_b, send_a = route(parent, child_parent, node_len, cached)
     path_a = lax.all_to_all(send_a, "group", 0, 0, tiled=True).reshape(-1, 2 * head)
@@ -400,21 +388,25 @@
         pltpu.VMEM((queries, 2 * head), jnp.float32),
     ]
     prefix = pltpu.with_memory_space_constraint(prefix, pltpu.HBM)
-    all_blocks = prefix.shape[0] // BLOCK
-    blocks = all_blocks - FIRST_BLOCKS
+    first_part = prefix.shape[0] // PART - FIRST_PARTS
+    block = first_part * PART // MIDDLE_STEPS
     anywhere = pl.BlockSpec(memory_space=pl.ANY)
     state_scratch = [pltpu.VMEM(s.shape, s.dtype) for s in state]
     stat, acc = pl.pallas_call(
         functools.partial(first_kernel, scale),
-        grid=(FIRST_BLOCKS,),
+        grid=(1,),
         out_shape=state,
-        in_specs=[spec(decode_q.shape), pl.BlockSpec((BLOCK, 2 * head), lambda i: (i, 0))],
+        in_specs=[spec(decode_q.shape)]
+        + [
+            pl.BlockSpec((PART, 2 * head), lambda i, part=first_part + k: (part, 0))
+            for k in range(FIRST_PARTS)
+        ],
         out_specs=[spec(s.shape) for s in state],
         scratch_shapes=scratch,
         compiler_params=params,
-        cost_estimate=attention_cost(queries, head, FIRST_BLOCKS * BLOCK),
+        cost_estimate=attention_cost(queries, head, FIRST_PARTS * PART),
         name="attend_first",
-    )(decode_q, prefix)
+    )(decode_q, *[prefix] * FIRST_PARTS)
 
     send_b = project_fresh(pick, hidden, key_value_weight, key_value_bias, cached)
     path_b = lax.all_to_all(send_b, "group", 0, 0, tiled=True).reshape(-1, 2 * head)
@@ -422,46 +414,41 @@
     path_b = pltpu.with_memory_space_constraint(path_b, pltpu.VMEM)
     stat, acc = (pltpu.with_memory_space_constraint(a, pltpu.HBM) for a in (stat, acc))
 
-    stat, acc = pl.pallas_call(
-        functools.partial(middle_kernel, scale, steps, blocks),
-        grid=(blocks + 1,),
-        out_shape=state,
+    on_chip = pl.BlockSpec(memory_space=pltpu.VMEM)
+    kept = (pltpu.VMEM((queries, head), jnp.float32), pltpu.VMEM((queries, 2 * head), jnp.float32))
+    maximum, total = pl.pallas_call(
+        functools.partial(middle_kernel, scale, steps, MIDDLE_STEPS),
+        grid=(MIDDLE_STEPS + 1,),
+        out_shape=kept,
         in_specs=[
             spec(decode_q.shape),
-            pl.BlockSpec(
-                (BLOCK, 2 * head), lambda i: (jnp.minimum(i + FIRST_BLOCKS, all_blocks - 1), 0)
-            ),
+            pl.BlockSpec((block, 2 * head), lambda i: (jnp.minimum(i, MIDDLE_STEPS - 1), 0)),
             anywhere,
             spec(bias_a.shape),
             spec(own.shape),
             anywhere,
             anywhere,
         ],
-        out_specs=[spec(s.shape) for s in state],
-        scratch_shapes=scratch
+        out_specs=[on_chip, on_chip],
+        scratch_shapes=scratch[:1]
         + state_scratch
         + [pltpu.VMEM(path_a.shape, path_a.dtype), pltpu.SemaphoreType.DMA((3,))],
         compiler_params=params,
-        cost_estimate=attention_cost(queries, head, blocks * BLOCK + path_a.shape[0]),
+        cost_estimate=attention_cost(queries, head, MIDDLE_STEPS * block + path_a.shape[0]),
         name="attend_middle",
     )(decode_q, prefix, path_a, bias_a, own, stat, acc)
+    maximum, total = (pltpu.with_memory_space_constraint(a, pltpu.VMEM) for a in (maximum, total))
 
     return pl.pallas_call(
         functools.partial(last_kernel, scale),
         out_shape=jax.ShapeDtypeStruct(decode_q.shape, jnp.bfloat16),
-        in_specs=[
-            spec(decode_q.shape),
-            pl.BlockSpec(memory_space=pltpu.VMEM),
-            spec(bias_b.shape),
-            spec(state[0].shape),
-            spec(state[1].shape),
-        ],
+        in_specs=[spec(decode_q.shape), on_chip, spec(bias_b.shape), on_chip, on_chip],
         out_specs=spec(decode_q.shape),
         scratch_shapes=scratch,
         compiler_params=params,
         cost_estimate=attention_cost(queries, head, path_b.shape[0]),
         name="attend_last",
-    )(decode_q, path_b, bias_b, stat, acc)
+    )(decode_q, path_b, bias_b, maximum, total)
 
 
 def solution(mesh):

time: 74.5 us -> 82.6 us (1.11)
  waiting for transfers between devices: 8.13 us -> 15.5 us
  starting transfers between devices: 25.1 us -> 27.1 us
  Pallas kernels: 40.9 us -> 39.5 us
    ppermute x7, waiting for transfers between devices: 7.68 us -> 15.5 us  [moved(): return lax.ppermute(block, 'tp', [(t, t ^ distance) for t in range(tp)])]
    pallas_call x2, Pallas kernels: 29.8 us -> 28.8 us  [the longest x1 18.3 us: per_device(): pl.pallas_call(functools.partial(middle_kernel, scale, steps, MIDDLE_STEP...]
    ppermute x7, starting transfers between devices: 9.89 us -> 10.7 us  [moved(): return lax.ppermute(block, 'tp', [(t, t ^ distance) for t in range(tp)])]
  transfers between devices with their start and end apart: 9 -> 9, of which waited for: 4 -> 2; matrix products, arithmetic and copies ran while one was open for 0% -> 0% of each run, Pallas kernels for 49% -> 38%
where the time goes in v5:
time: 82.6 us; the launch traced here: 82.3 us
  Pallas kernels  39.5 us (48%)
  starting transfers between devices  27.1 us (33%)
  waiting for transfers between devices  15.5 us (19%)
    pallas_call x1, Pallas kernels, per_device(): pl.pallas_call(functools.partial(middle_kernel, scale, steps, MIDDLE_STEP...  18.3 us
    ppermute x7, waiting for transfers between devices, moved(): return lax.ppermute(block, 'tp', [(t, t ^ distance) for t in range(tp)])  15.5 us
    ppermute x7, starting transfers between devices, moved(): return lax.ppermute(block, 'tp', [(t, t ^ distance) for t in range(tp)])  10.7 us
    pallas_call x1, Pallas kernels, per_device(): pl.pallas_call(functools.partial(first_kernel, scale), grid=(1,), out_sha...  10.4 us
    all_to_all x1, starting transfers between devices, per_device(): lax.all_to_all(send_a, 'group', 0, 0, tiled=True).reshape(-1, 2 * head)  8.45 us
    all_to_all x1, starting transfers between devices, per_device(): lax.all_to_all(send_b, 'group', 0, 0, tiled=True).reshape(-1, 2 * head)  7.94 us
    pallas_call x1, Pallas kernels, per_device(): pl.pallas_call(functools.partial(last_kernel, scale), out_shape=jax.Shape...  4.5 us
    pallas_call x1, Pallas kernels, route(): pl.pallas_call(functools.partial(route_kernel, groups), out_shape=out, in...  3.7 us
  transfers between devices with their start and end apart: 9, of which 2 were waited for; matrix products, arithmetic and copies ran while one was open for 0% of the time, Pallas kernels for 38%

profile of v5, /device:TPU:1, one launch (start us, length us, event | category | flops | bytes accessed | tf_op | source)
XLA Modules:
  0.0 82.3 jit_solution(8964167635172001541)
XLA Ops:
  0.0 3.7 %route.1 = (s32[16,128]{1,0:T(8,128)}, f32[16,128]{1,0:T(8,128)}, f32[16,128]{1,0:T(8,128)}, bf16[16,2,64,256]{3,2,1,0:T(8,128)(2,1)}) custom-call(s32[4,128]{1,0:T(4,128)} %bitcast.14, s32[16]{0:T(128)} %child_ref.1, s32[4,128]{1,0:T(4,128)} %bitcast.15, bf16[30,64,256]{2,1,0:T(8,128)(2,1)} %bitcast.7), custom_call_target="tpu_custom_call" | custom-call | flops 16777216 | bytes 2097152 | tf_op jit(solution)/shard_map/route/pallas_call | solution.py:131
  3.7 8.4 %all-to-all-start.1 = ((bf16[16,2,64,256]{3,2,1,0:T(8,128)(2,1)}), bf16[16,2,64,256]{3,2,1,0:T(8,128)(2,1)}, u32[]{:S(2)}, u32[]{:S(2)}) async-start(bf16[16,2,64,256]{3,2,1,0:T(8,128)(2,1)} %get-tuple-element.15), calls=%async_computation.1 | async-start | bytes 2097152 | tf_op jit(solution)/shard_map/all_to_all | solution.py:381
  12.2 0.3 collective-permute-start
  12.5 3.8 %collective-permute-start.3 = (bf16[16,8192]{1,0:T(8,128)(2,1)}, bf16[16,8192]{1,0:T(8,128)(2,1)S(1)}, u32[]{:S(2)}, u32[]{:S(2)}) collective-permute-start(bf16[16,8192]{1,0:T(8,128)(2,1)} %refs_0_.1), channel_id=1, source_target_pairs={{0,6},{1,7},{2,4},{3,5},{4,2},{5,3},{6,0},{7,1},{8,14},{9,15},{10,... | collective-permute-start | bytes 786440 | tf_op jit(solution)/shard_map/ppermute | solution.py:372
  16.2 0.0 collective-permute-start.1
  16.2 2.1 %collective-permute-start.5 = (bf16[16,8192]{1,0:T(8,128)(2,1)}, bf16[16,8192]{1,0:T(8,128)(2,1)S(1)}, u32[]{:S(2)}, u32[]{:S(2)}) collective-permute-start(bf16[16,8192]{1,0:T(8,128)(2,1)} %refs_0_.1), channel_id=1, source_target_pairs={{0,5},{1,4},{2,7},{3,6},{4,1},{5,0},{6,3},{7,2},{8,13},{9,12},{10,... | collective-permute-start | bytes 786440 | tf_op jit(solution)/shard_map/ppermute | solution.py:372
  18.3 12.3 %collective-permute-done.refs_1_ = bf16[16,8192]{1,0:T(8,128)(2,1)S(1)} collective-permute-done((bf16[16,8192]{1,0:T(8,128)(2,1)}, bf16[16,8192]{1,0:T(8,128)(2,1)S(1)}, u32[]{:S(2)}, u32[]{:S(2)}) %collective-permute-start) | collective-permute-done | bytes 262176 | tf_op jit(solution)/shard_map/ppermute | solution.py:372
  30.6 1.6 %collective-permute-start.2 = (bf16[16,8192]{1,0:T(8,128)(2,1)S(1)}, bf16[16,8192]{1,0:T(8,128)(2,1)S(1)}, u32[]{:S(2)}, u32[]{:S(2)}) collective-permute-start(bf16[16,8192]{1,0:T(8,128)(2,1)S(1)} %collective-permute-done.refs_1_), channel_id=1, source_target_pairs={{0,2},{1,3},{2,0},{3,1},{4,6},{5,7},{6,4},{7,5},{8,10},{9,11},{10,... | collective-permute-start | bytes 786440 | tf_op jit(solution)/shard_map/ppermute | solution.py:372
  32.2 2.2 %collective-permute-start.6 = (bf16[16,8192]{1,0:T(8,128)(2,1)S(1)}, bf16[16,8192]{1,0:T(8,128)(2,1)S(1)}, u32[]{:S(2)}, u32[]{:S(2)}) collective-permute-start(bf16[16,8192]{1,0:T(8,128)(2,1)S(1)} %collective-permute-done.refs_1_), channel_id=1, source_target_pairs={{0,6},{1,7},{2,4},{3,5},{4,2},{5,3},{6,0},{7,1},{8,14},{9,15},{10,... | collective-permute-start | bytes 786440 | tf_op jit(solution)/shard_map/ppermute | solution.py:372
  34.5 0.0 collective-permute-done.3.refs_6_
  34.5 0.7 collective-permute-start.4
  35.2 0.0 copy-start
  35.2 0.0 copy-start.1
  35.2 0.0 copy-start.2
  35.2 0.0 copy-start.4
  35.2 10.4 %attend_first.1 = (f32[1024,128]{1,0:T(8,128)}, f32[1024,128]{1,0:T(8,128)}) custom-call(bf16[128,1024]{1,0:T(8,128)(2,1)} %q_ref.5, bf16[16384,256]{1,0:T(8,128)(2,1)} %bitcast.10, bf16[16384,256]{1,0:T(8,128)(2,1)} %bitcast.11, bf16[16384,256]{1,0:T(8,128)(2,1)} %bitcast.12), custom_call_target="tpu_custom_call" | custom-call | flops 6442450944 | bytes 3145728 | tf_op jit(solution)/shard_map/attend_first/pallas_call | solution.py:395
  45.7 0.0 collective-permute-done.1.refs_2_
  45.7 0.0 collective-permute-done.5.refs_5_
  45.7 0.0 collective-permute-done.2.refs_3_
  45.7 0.0 collective-permute-done.6.refs_7_
  45.7 3.2 %collective-permute-done.4.refs_4_ = bf16[16,8192]{1,0:T(8,128)(2,1)S(1)} collective-permute-done((bf16[16,8192]{1,0:T(8,128)(2,1)S(1)}, bf16[16,8192]{1,0:T(8,128)(2,1)S(1)}, u32[]{:S(2)}, u32[]{:S(2)}) %collective-permute-start.4) | collective-permute-done | bytes 262176 | tf_op jit(solution)/shard_map/ppermute | solution.py:372
  48.9 0.0 copy-done
  48.9 0.0 copy-done.1
  48.9 0.0 copy-done.2
  48.9 0.0 copy-done.3
  48.9 0.0 copy-done.4
  48.9 2.5 %fresh.1 = bf16[16,2,64,256]{3,2,1,0:T(8,128)(2,1)} custom-call(s32[16,128]{1,0:T(8,128)S(1)} %copy-done.3, bf16[16,8192]{1,0:T(8,128)(2,1)S(1)} %copy-done.2, bf16[16,8192]{1,0:T(8,128)(2,1)S(1)} %collective-permute-done.refs_1_, bf16[16,8192]{1,0:T(8,128)(2,1)S(1)} %collective-permute-done.1.refs_2_, bf16[16,8192]{1,0:T(8,128)(2,1)S(1)} %collective-permute-done.2.refs_3_, ...), custom_call_target="tpu_custom_call" | custom-call | flops 536870912 | bytes 8388608 | tf_op jit(solution)/shard_map/fresh/pallas_call | solution.py:177
  51.4 0.0 all-to-all-done.1
  51.5 7.9 %all-to-all-start = ((bf16[16,2,64,256]{3,2,1,0:T(8,128)(2,1)}), bf16[16,2,64,256]{3,2,1,0:T(8,128)(2,1)S(1)}, u32[]{:S(2)}, u32[]{:S(2)}) async-start(bf16[16,2,64,256]{3,2,1,0:T(8,128)(2,1)} %fresh.1), calls=%async_computation | async-start | bytes 2097152 | tf_op jit(solution)/shard_map/all_to_all | solution.py:412
  59.4 18.3 %attend_middle.1 = (f32[1024,128]{1,0:T(8,128)S(1)}, f32[1024,256]{1,0:T(8,128)S(1)}) custom-call(bf16[128,1024]{1,0:T(8,128)(2,1)} %q_ref.5, bf16[16384,256]{1,0:T(8,128)(2,1)} %bitcast.13, bf16[2048,256]{1,0:T(8,128)(2,1)} %bitcast.5.path_ref, f32[16,128]{1,0:T(8,128)} %get-tuple-element.16.bias_ref, bf16[128,256]{1,0:T(8,128)(2,1)} %bitcast.16, ...), custom_call_target="tpu_custom_call" | custom-call | flops 12884901888 | bytes 6291456 | tf_op jit(solution)/shard_map/attend_middle/pallas_call | solution.py:419
  77.7 0.0 all-to-all-done
  77.8 4.5 %attend_last.1 = bf16[128,1024]{1,0:T(8,128)(2,1)} custom-call(bf16[128,1024]{1,0:T(8,128)(2,1)} %q_ref.5, bf16[2048,256]{1,0:T(8,128)(2,1)S(1)} %bitcast.9, f32[16,128]{1,0:T(8,128)} %get-tuple-element.14.bias_ref, f32[1024,128]{1,0:T(8,128)S(1)} %get-tuple-element.19.max_in, f32[1024,256]{1,0:T(8,128)S(1)} %get-tuple-element.20.total_in), custom_call_target="tpu_custom_call" | custom-call | flops 2147483648 | bytes 1048576 | tf_op jit(solution)/shard_map/attend_last/pallas_call | solution.py:442
  (1 shorter events, 0.0 us)
Async XLA Ops:
  3.7 47.7 %all-to-all-start.1 = ((bf16[16,2,64,256]{3,2,1,0:T(8,128)(2,1)}), bf16[16,2,64,256]{3,2,1,0:T(8,128)(2,1)}, u32[]{:S(2)}, u32[]{:S(2)}) async-start(bf16[16,2,64,256]{3,2,1,0:T(8,128)(2,1)} %get-tuple-element.15), calls=%async_computation.1 | async-start | bytes 2097152 | tf_op jit(solution)/shard_map/all_to_all | solution.py:381
  12.2 18.4 %collective-permute-start = (bf16[16,8192]{1,0:T(8,128)(2,1)}, bf16[16,8192]{1,0:T(8,128)(2,1)S(1)}, u32[]{:S(2)}, u32[]{:S(2)}) collective-permute-start(bf16[16,8192]{1,0:T(8,128)(2,1)} %refs_0_.1), channel_id=1, source_target_pairs={{0,1},{1,0},{2,3},{3,2},{4,5},{5,4},{6,7},{7,6},{8,9},{9,8},{10,11... | collective-permute-start | bytes 786440 | tf_op jit(solution)/shard_map/ppermute | solution.py:372
  12.5 22.0 %collective-permute-start.3 = (bf16[16,8192]{1,0:T(8,128)(2,1)}, bf16[16,8192]{1,0:T(8,128)(2,1)S(1)}, u32[]{:S(2)}, u32[]{:S(2)}) collective-permute-start(bf16[16,8192]{1,0:T(8,128)(2,1)} %refs_0_.1), channel_id=1, source_target_pairs={{0,6},{1,7},{2,4},{3,5},{4,2},{5,3},{6,0},{7,1},{8,14},{9,15},{10,... | collective-permute-start | bytes 786440 | tf_op jit(solution)/shard_map/ppermute | solution.py:372
  16.2 29.4 %collective-permute-start.1 = (bf16[16,8192]{1,0:T(8,128)(2,1)}, bf16[16,8192]{1,0:T(8,128)(2,1)S(1)}, u32[]{:S(2)}, u32[]{:S(2)}) collective-permute-start(bf16[16,8192]{1,0:T(8,128)(2,1)} %refs_0_.1), channel_id=1, source_target_pairs={{0,2},{1,3},{2,0},{3,1},{4,6},{5,7},{6,4},{7,5},{8,10},{9,11},{10,... | collective-permute-start | bytes 786440 | tf_op jit(solution)/shard_map/ppermute | solution.py:372
  16.2 29.4 %collective-permute-start.5 = (bf16[16,8192]{1,0:T(8,128)(2,1)}, bf16[16,8192]{1,0:T(8,128)(2,1)S(1)}, u32[]{:S(2)}, u32[]{:S(2)}) collective-permute-start(bf16[16,8192]{1,0:T(8,128)(2,1)} %refs_0_.1), channel_id=1, source_target_pairs={{0,5},{1,4},{2,7},{3,6},{4,1},{5,0},{6,3},{7,2},{8,13},{9,12},{10,... | collective-permute-start | bytes 786440 | tf_op jit(solution)/shard_map/ppermute | solution.py:372
  30.6 15.1 %collective-permute-start.2 = (bf16[16,8192]{1,0:T(8,128)(2,1)S(1)}, bf16[16,8192]{1,0:T(8,128)(2,1)S(1)}, u32[]{:S(2)}, u32[]{:S(2)}) collective-permute-start(bf16[16,8192]{1,0:T(8,128)(2,1)S(1)} %collective-permute-done.refs_1_), channel_id=1, source_target_pairs={{0,2},{1,3},{2,0},{3,1},{4,6},{5,7},{6,4},{7,5},{8,10},{9,11},{10,... | collective-permute-start | bytes 786440 | tf_op jit(solution)/shard_map/ppermute | solution.py:372
  32.2 13.5 %collective-permute-start.6 = (bf16[16,8192]{1,0:T(8,128)(2,1)S(1)}, bf16[16,8192]{1,0:T(8,128)(2,1)S(1)}, u32[]{:S(2)}, u32[]{:S(2)}) collective-permute-start(bf16[16,8192]{1,0:T(8,128)(2,1)S(1)} %collective-permute-done.refs_1_), channel_id=1, source_target_pairs={{0,6},{1,7},{2,4},{3,5},{4,2},{5,3},{6,0},{7,1},{8,14},{9,15},{10,... | collective-permute-start | bytes 786440 | tf_op jit(solution)/shard_map/ppermute | solution.py:372
  34.5 14.4 %collective-permute-start.4 = (bf16[16,8192]{1,0:T(8,128)(2,1)S(1)}, bf16[16,8192]{1,0:T(8,128)(2,1)S(1)}, u32[]{:S(2)}, u32[]{:S(2)}) collective-permute-start(bf16[16,8192]{1,0:T(8,128)(2,1)S(1)} %collective-permute-done.3.refs_6_), channel_id=1, source_target_pairs={{0,2},{1,3},{2,0},{3,1},{4,6},{5,7},{6,4},{7,5},{8,10},{9,11},{10,... | collective-permute-start | bytes 786440 | tf_op jit(solution)/shard_map/ppermute | solution.py:372
  35.2 13.7 %copy-start = (bf16[8192,256]{1,0:T(8,128)(2,1)S(1)}, bf16[8192,256]{1,0:T(8,128)(2,1)}, u32[]{:S(2)}) copy-start(bf16[8192,256]{1,0:T(8,128)(2,1)} %refs_8_.1) | copy-start | bytes 12582916
  35.2 13.7 %copy-start.1 = (bf16[1,30,64,256]{3,2,1,0:T(8,128)(2,1)S(1)}, bf16[1,30,64,256]{3,2,1,0:T(8,128)(2,1)}, u32[]{:S(2)}) copy-start(bf16[1,30,64,256]{3,2,1,0:T(8,128)(2,1)} %param.11) | copy-start | bytes 2949124
  35.2 13.7 %copy-start.2 = (bf16[16,8192]{1,0:T(8,128)(2,1)S(1)}, bf16[16,8192]{1,0:T(8,128)(2,1)}, u32[]{:S(2)}) copy-start(bf16[16,8192]{1,0:T(8,128)(2,1)} %refs_0_.1) | copy-start | bytes 786436
  35.2 13.7 %copy-start.3 = (s32[16,128]{1,0:T(8,128)S(1)}, s32[16,128]{1,0:T(8,128)}, u32[]{:S(2)}) copy-start(s32[16,128]{1,0:T(8,128)} %get-tuple-element.13.pick_ref) | copy-start | bytes 24580
  35.2 13.7 %copy-start.4 = (bf16[256]{0:T(256)(128)(2,1)S(1)}, bf16[256]{0:T(256)(128)(2,1)}, u32[]{:S(2)}) copy-start(bf16[256]{0:T(256)(128)(2,1)} %refs_9_.1) | copy-start | bytes 1540
  51.5 26.3 %all-to-all-start = ((bf16[16,2,64,256]{3,2,1,0:T(8,128)(2,1)}), bf16[16,2,64,256]{3,2,1,0:T(8,128)(2,1)S(1)}, u32[]{:S(2)}, u32[]{:S(2)}) async-start(bf16[16,2,64,256]{3,2,1,0:T(8,128)(2,1)} %fresh.1), calls=%async_computation | async-start | bytes 2097152 | tf_op jit(solution)/shard_map/all_to_all | solution.py:412

commit v6 on v5

--- a/solution.py
+++ b/solution.py
@@ -294,12 +294,16 @@
 
 
 def first_kernel(scale, q_ref, *refs):
-    prefix_refs, (stat_ref, acc_ref, query, maximum, total) = refs[:FIRST_PARTS], refs[FIRST_PARTS:]
+    prefix_refs = refs[:FIRST_PARTS]
+    weight_ref, stat_ref, acc_ref, weight_v, query, maximum, total, sem = refs[FIRST_PARTS:]
+    fetch = pltpu.make_async_copy(weight_ref, weight_v, sem)
+    fetch.start()
     load_query(q_ref, query)
     empty_state(maximum, total)
     pieces = [piece for ref in prefix_refs for piece in plain_pieces(ref)]
     take_keys(query, maximum, total, pieces, scale)
     put_state(maximum, total, stat_ref, acc_ref)
+    fetch.wait()
 
 
 def middle_kernel(scale, steps, blocks, q_ref, prefix_ref, path_ref, bias_ref, own_ref, stat_in, acc_in, maximum, total, query, stat_v, acc_v, path_v, sem):
@@ -392,23 +396,26 @@
     block = first_part * PART // MIDDLE_STEPS
     anywhere = pl.BlockSpec(memory_space=pl.ANY)
     state_scratch = [pltpu.VMEM(s.shape, s.dtype) for s in state]
-    stat, acc = pl.pallas_call(
+    weight = key_value_weight
+    stat, acc, weight = pl.pallas_call(
         functools.partial(first_kernel, scale),
         grid=(1,),
-        out_shape=state,
+        out_shape=(*state, pltpu.VMEM(weight.shape, weight.dtype)),
         in_specs=[spec(decode_q.shape)]
         + [
             pl.BlockSpec((PART, 2 * head), lambda i, part=first_part + k: (part, 0))
             for k in range(FIRST_PARTS)
-        ],
-        out_specs=[spec(s.shape) for s in state],
-        scratch_shapes=scratch,
+        ]
+        + [anywhere],
+        out_specs=[spec(s.shape) for s in state] + [pl.BlockSpec(memory_space=pltpu.VMEM)],
+        scratch_shapes=scratch + [pltpu.SemaphoreType.DMA],
         compiler_params=params,
         cost_estimate=attention_cost(queries, head, FIRST_PARTS * PART),
         name="attend_first",
-    )(decode_q, *[prefix] * FIRST_PARTS)
-
-    send_b = project_fresh(pick, hidden, key_value_weight, key_value_bias, cached)
+    )(decode_q, *[prefix] * FIRST_PARTS, pltpu.with_memory_space_constraint(weight, pltpu.HBM))
+    weight = pltpu.with_memory_space_constraint(weight, pltpu.VMEM)
+
+    send_b = project_fresh(pick, hidden, weight, key_value_bias, cached)
     path_b = lax.all_to_all(send_b, "group", 0, 0, tiled=True).reshape(-1, 2 * head)
     path_a = pltpu.with_memory_space_constraint(path_a, pltpu.HBM)
     path_b = pltpu.with_memory_space_constraint(path_b, pltpu.VMEM)

time: 82.6 us -> 82.5 us (level)
  no operation moved by 1% of the time
where the time goes in v6:
time: 82.5 us; the launch traced here: 82.2 us
  Pallas kernels  39.5 us (48%)
  starting transfers between devices  27.1 us (33%)
  waiting for transfers between devices  15.5 us (19%)
    pallas_call x1, Pallas kernels, per_device(): pl.pallas_call(functools.partial(middle_kernel, scale, steps, MIDDLE_STEP...  18.3 us
    ppermute x7, waiting for transfers between devices, moved(): return lax.ppermute(block, 'tp', [(t, t ^ distance) for t in range(tp)])  15.5 us
    ppermute x7, starting transfers between devices, moved(): return lax.ppermute(block, 'tp', [(t, t ^ distance) for t in range(tp)])  10.7 us
    pallas_call x1, Pallas kernels, per_device(): pl.pallas_call(functools.partial(first_kernel, scale), grid=(1,), out_sha...  10.4 us
    all_to_all x1, starting transfers between devices, per_device(): lax.all_to_all(send_a, 'group', 0, 0, tiled=True).reshape(-1, 2 * head)  8.45 us
    all_to_all x1, starting transfers between devices, per_device(): lax.all_to_all(send_b, 'group', 0, 0, tiled=True).reshape(-1, 2 * head)  7.93 us
    pallas_call x1, Pallas kernels, per_device(): pl.pallas_call(functools.partial(last_kernel, scale), out_shape=jax.Shape...  4.5 us
    pallas_call x1, Pallas kernels, route(): pl.pallas_call(functools.partial(route_kernel, groups), out_shape=out, in...  3.7 us
  transfers between devices with their start and end apart: 9, of which 2 were waited for; matrix products, arithmetic and copies ran while one was open for 0% of the time, Pallas kernels for 38%

profile of v6, /device:TPU:1, one launch (start us, length us, event | category | flops | bytes accessed | tf_op | source)
XLA Modules:
  0.0 82.2 jit_solution(16439591098771464005)
XLA Ops:
  0.0 3.7 %route.1 = (s32[16,128]{1,0:T(8,128)}, f32[16,128]{1,0:T(8,128)}, f32[16,128]{1,0:T(8,128)}, bf16[16,2,64,256]{3,2,1,0:T(8,128)(2,1)}) custom-call(s32[4,128]{1,0:T(4,128)} %bitcast.14, s32[16]{0:T(128)} %child_ref.1, s32[4,128]{1,0:T(4,128)} %bitcast.15, bf16[30,64,256]{2,1,0:T(8,128)(2,1)} %bitcast.7), custom_call_target="tpu_custom_call" | custom-call | flops 16777216 | bytes 2097152 | tf_op jit(solution)/shard_map/route/pallas_call | solution.py:131
  3.7 8.4 %all-to-all-start.1 = ((bf16[16,2,64,256]{3,2,1,0:T(8,128)(2,1)}), bf16[16,2,64,256]{3,2,1,0:T(8,128)(2,1)}, u32[]{:S(2)}, u32[]{:S(2)}) async-start(bf16[16,2,64,256]{3,2,1,0:T(8,128)(2,1)} %get-tuple-element.17), calls=%async_computation.1 | async-start | bytes 2097152 | tf_op jit(solution)/shard_map/all_to_all | solution.py:385
  12.2 0.3 collective-permute-start
  12.5 3.8 %collective-permute-start.3 = (bf16[16,8192]{1,0:T(8,128)(2,1)}, bf16[16,8192]{1,0:T(8,128)(2,1)S(1)}, u32[]{:S(2)}, u32[]{:S(2)}) collective-permute-start(bf16[16,8192]{1,0:T(8,128)(2,1)} %refs_0_.1), channel_id=1, source_target_pairs={{0,6},{1,7},{2,4},{3,5},{4,2},{5,3},{6,0},{7,1},{8,14},{9,15},{10,... | collective-permute-start | bytes 786440 | tf_op jit(solution)/shard_map/ppermute | solution.py:376
  16.2 0.0 collective-permute-start.1
  16.2 2.1 %collective-permute-start.5 = (bf16[16,8192]{1,0:T(8,128)(2,1)}, bf16[16,8192]{1,0:T(8,128)(2,1)S(1)}, u32[]{:S(2)}, u32[]{:S(2)}) collective-permute-start(bf16[16,8192]{1,0:T(8,128)(2,1)} %refs_0_.1), channel_id=1, source_target_pairs={{0,5},{1,4},{2,7},{3,6},{4,1},{5,0},{6,3},{7,2},{8,13},{9,12},{10,... | collective-permute-start | bytes 786440 | tf_op jit(solution)/shard_map/ppermute | solution.py:376
  18.3 12.3 %collective-permute-done.refs_1_ = bf16[16,8192]{1,0:T(8,128)(2,1)S(1)} collective-permute-done((bf16[16,8192]{1,0:T(8,128)(2,1)}, bf16[16,8192]{1,0:T(8,128)(2,1)S(1)}, u32[]{:S(2)}, u32[]{:S(2)}) %collective-permute-start) | collective-permute-done | bytes 262176 | tf_op jit(solution)/shard_map/ppermute | solution.py:376
  30.6 1.6 %collective-permute-start.2 = (bf16[16,8192]{1,0:T(8,128)(2,1)S(1)}, bf16[16,8192]{1,0:T(8,128)(2,1)S(1)}, u32[]{:S(2)}, u32[]{:S(2)}) collective-permute-start(bf16[16,8192]{1,0:T(8,128)(2,1)S(1)} %collective-permute-done.refs_1_), channel_id=1, source_target_pairs={{0,2},{1,3},{2,0},{3,1},{4,6},{5,7},{6,4},{7,5},{8,10},{9,11},{10,... | collective-permute-start | bytes 786440 | tf_op jit(solution)/shard_map/ppermute | solution.py:376
  32.2 2.2 %collective-permute-start.6 = (bf16[16,8192]{1,0:T(8,128)(2,1)S(1)}, bf16[16,8192]{1,0:T(8,128)(2,1)S(1)}, u32[]{:S(2)}, u32[]{:S(2)}) collective-permute-start(bf16[16,8192]{1,0:T(8,128)(2,1)S(1)} %collective-permute-done.refs_1_), channel_id=1, source_target_pairs={{0,6},{1,7},{2,4},{3,5},{4,2},{5,3},{6,0},{7,1},{8,14},{9,15},{10,... | collective-permute-start | bytes 786440 | tf_op jit(solution)/shard_map/ppermute | solution.py:376
  34.5 0.0 collective-permute-done.3.refs_6_
  34.5 0.7 collective-permute-start.4
  35.2 0.0 copy-start
  35.2 0.0 copy-start.1
  35.2 0.0 copy-start.2
  35.2 0.0 copy-start.3
  35.2 10.4 %attend_first.1 = (f32[1024,128]{1,0:T(8,128)}, f32[1024,128]{1,0:T(8,128)}, bf16[8192,256]{1,0:T(8,128)(2,1)S(1)}) custom-call(bf16[128,1024]{1,0:T(8,128)(2,1)} %q_ref.5, bf16[16384,256]{1,0:T(8,128)(2,1)} %bitcast.10, bf16[16384,256]{1,0:T(8,128)(2,1)} %bitcast.11, bf16[16384,256]{1,0:T(8,128)(2,1)} %bitcast.12, bf16[8192,256]{1,0:T(8,128)(2,1)} %refs_3_.1), custom_call_target="tpu_custom_call" | custom-call | flops 6442450944 | bytes 3145728 | tf_op jit(solution)/shard_map/attend_first/pallas_call | solution.py:400
  45.6 0.0 collective-permute-done.1.refs_2_
  45.6 0.0 collective-permute-done.5.refs_5_
  45.6 0.0 collective-permute-done.2.refs_3_
  45.7 0.0 collective-permute-done.6.refs_7_
  45.7 3.2 %collective-permute-done.4.refs_4_ = bf16[16,8192]{1,0:T(8,128)(2,1)S(1)} collective-permute-done((bf16[16,8192]{1,0:T(8,128)(2,1)S(1)}, bf16[16,8192]{1,0:T(8,128)(2,1)S(1)}, u32[]{:S(2)}, u32[]{:S(2)}) %collective-permute-start.4) | collective-permute-done | bytes 262176 | tf_op jit(solution)/shard_map/ppermute | solution.py:376
  48.9 0.0 copy-done
  48.9 0.0 copy-done.1
  48.9 0.0 copy-done.2
  48.9 0.0 copy-done.3
  48.9 2.5 %fresh.1 = bf16[16,2,64,256]{3,2,1,0:T(8,128)(2,1)} custom-call(s32[16,128]{1,0:T(8,128)S(1)} %copy-done.2, bf16[16,8192]{1,0:T(8,128)(2,1)S(1)} %copy-done.1, bf16[16,8192]{1,0:T(8,128)(2,1)S(1)} %collective-permute-done.refs_1_, bf16[16,8192]{1,0:T(8,128)(2,1)S(1)} %collective-permute-done.1.refs_2_, bf16[16,8192]{1,0:T(8,128)(2,1)S(1)} %collective-permute-done.2.refs_3_, ...), custom_call_target="tpu_custom_call" | custom-call | flops 536870912 | bytes 8388608 | tf_op jit(solution)/shard_map/fresh/pallas_call | solution.py:177
  51.4 0.0 all-to-all-done.1
  51.4 7.9 %all-to-all-start = ((bf16[16,2,64,256]{3,2,1,0:T(8,128)(2,1)}), bf16[16,2,64,256]{3,2,1,0:T(8,128)(2,1)S(1)}, u32[]{:S(2)}, u32[]{:S(2)}) async-start(bf16[16,2,64,256]{3,2,1,0:T(8,128)(2,1)} %fresh.1), calls=%async_computation | async-start | bytes 2097152 | tf_op jit(solution)/shard_map/all_to_all | solution.py:419
  59.4 18.3 %attend_middle.1 = (f32[1024,128]{1,0:T(8,128)S(1)}, f32[1024,256]{1,0:T(8,128)S(1)}) custom-call(bf16[128,1024]{1,0:T(8,128)(2,1)} %q_ref.5, bf16[16384,256]{1,0:T(8,128)(2,1)} %bitcast.13, bf16[2048,256]{1,0:T(8,128)(2,1)} %bitcast.5.path_ref, f32[16,128]{1,0:T(8,128)} %get-tuple-element.18.bias_ref, bf16[128,256]{1,0:T(8,128)(2,1)} %bitcast.16, ...), custom_call_target="tpu_custom_call" | custom-call | flops 12884901888 | bytes 6291456 | tf_op jit(solution)/shard_map/attend_middle/pallas_call | solution.py:426
  77.7 0.0 all-to-all-done
  77.7 4.5 %attend_last.1 = bf16[128,1024]{1,0:T(8,128)(2,1)} custom-call(bf16[128,1024]{1,0:T(8,128)(2,1)} %q_ref.5, bf16[2048,256]{1,0:T(8,128)(2,1)S(1)} %bitcast.9, f32[16,128]{1,0:T(8,128)} %get-tuple-element.16.bias_ref, f32[1024,128]{1,0:T(8,128)S(1)} %get-tuple-element.21.max_in, f32[1024,256]{1,0:T(8,128)S(1)} %get-tuple-element.22.total_in), custom_call_target="tpu_custom_call" | custom-call | flops 2147483648 | bytes 1048576 | tf_op jit(solution)/shard_map/attend_last/pallas_call | solution.py:449
Async XLA Ops:
  3.7 47.7 %all-to-all-start.1 = ((bf16[16,2,64,256]{3,2,1,0:T(8,128)(2,1)}), bf16[16,2,64,256]{3,2,1,0:T(8,128)(2,1)}, u32[]{:S(2)}, u32[]{:S(2)}) async-start(bf16[16,2,64,256]{3,2,1,0:T(8,128)(2,1)} %get-tuple-element.17), calls=%async_computation.1 | async-start | bytes 2097152 | tf_op jit(solution)/shard_map/all_to_all | solution.py:385
  12.2 18.4 %collective-permute-start = (bf16[16,8192]{1,0:T(8,128)(2,1)}, bf16[16,8192]{1,0:T(8,128)(2,1)S(1)}, u32[]{:S(2)}, u32[]{:S(2)}) collective-permute-start(bf16[16,8192]{1,0:T(8,128)(2,1)} %refs_0_.1), channel_id=1, source_target_pairs={{0,1},{1,0},{2,3},{3,2},{4,5},{5,4},{6,7},{7,6},{8,9},{9,8},{10,11... | collective-permute-start | bytes 786440 | tf_op jit(solution)/shard_map/ppermute | solution.py:376
  12.5 22.0 %collective-permute-start.3 = (bf16[16,8192]{1,0:T(8,128)(2,1)}, bf16[16,8192]{1,0:T(8,128)(2,1)S(1)}, u32[]{:S(2)}, u32[]{:S(2)}) collective-permute-start(bf16[16,8192]{1,0:T(8,128)(2,1)} %refs_0_.1), channel_id=1, source_target_pairs={{0,6},{1,7},{2,4},{3,5},{4,2},{5,3},{6,0},{7,1},{8,14},{9,15},{10,... | collective-permute-start | bytes 786440 | tf_op jit(solution)/shard_map/ppermute | solution.py:376
  16.2 29.4 %collective-permute-start.1 = (bf16[16,8192]{1,0:T(8,128)(2,1)}, bf16[16,8192]{1,0:T(8,128)(2,1)S(1)}, u32[]{:S(2)}, u32[]{:S(2)}) collective-permute-start(bf16[16,8192]{1,0:T(8,128)(2,1)} %refs_0_.1), channel_id=1, source_target_pairs={{0,2},{1,3},{2,0},{3,1},{4,6},{5,7},{6,4},{7,5},{8,10},{9,11},{10,... | collective-permute-start | bytes 786440 | tf_op jit(solution)/shard_map/ppermute | solution.py:376
  16.2 29.4 %collective-permute-start.5 = (bf16[16,8192]{1,0:T(8,128)(2,1)}, bf16[16,8192]{1,0:T(8,128)(2,1)S(1)}, u32[]{:S(2)}, u32[]{:S(2)}) collective-permute-start(bf16[16,8192]{1,0:T(8,128)(2,1)} %refs_0_.1), channel_id=1, source_target_pairs={{0,5},{1,4},{2,7},{3,6},{4,1},{5,0},{6,3},{7,2},{8,13},{9,12},{10,... | collective-permute-start | bytes 786440 | tf_op jit(solution)/shard_map/ppermute | solution.py:376
  30.6 15.1 %collective-permute-start.2 = (bf16[16,8192]{1,0:T(8,128)(2,1)S(1)}, bf16[16,8192]{1,0:T(8,128)(2,1)S(1)}, u32[]{:S(2)}, u32[]{:S(2)}) collective-permute-start(bf16[16,8192]{1,0:T(8,128)(2,1)S(1)} %collective-permute-done.refs_1_), channel_id=1, source_target_pairs={{0,2},{1,3},{2,0},{3,1},{4,6},{5,7},{6,4},{7,5},{8,10},{9,11},{10,... | collective-permute-start | bytes 786440 | tf_op jit(solution)/shard_map/ppermute | solution.py:376
  32.2 13.4 %collective-permute-start.6 = (bf16[16,8192]{1,0:T(8,128)(2,1)S(1)}, bf16[16,8192]{1,0:T(8,128)(2,1)S(1)}, u32[]{:S(2)}, u32[]{:S(2)}) collective-permute-start(bf16[16,8192]{1,0:T(8,128)(2,1)S(1)} %collective-permute-done.refs_1_), channel_id=1, source_target_pairs={{0,6},{1,7},{2,4},{3,5},{4,2},{5,3},{6,0},{7,1},{8,14},{9,15},{10,... | collective-permute-start | bytes 786440 | tf_op jit(solution)/shard_map/ppermute | solution.py:376
  34.5 14.4 %collective-permute-start.4 = (bf16[16,8192]{1,0:T(8,128)(2,1)S(1)}, bf16[16,8192]{1,0:T(8,128)(2,1)S(1)}, u32[]{:S(2)}, u32[]{:S(2)}) collective-permute-start(bf16[16,8192]{1,0:T(8,128)(2,1)S(1)} %collective-permute-done.3.refs_6_), channel_id=1, source_target_pairs={{0,2},{1,3},{2,0},{3,1},{4,6},{5,7},{6,4},{7,5},{8,10},{9,11},{10,... | collective-permute-start | bytes 786440 | tf_op jit(solution)/shard_map/ppermute | solution.py:376
  35.2 13.7 %copy-start = (bf16[1,30,64,256]{3,2,1,0:T(8,128)(2,1)S(1)}, bf16[1,30,64,256]{3,2,1,0:T(8,128)(2,1)}, u32[]{:S(2)}) copy-start(bf16[1,30,64,256]{3,2,1,0:T(8,128)(2,1)} %param.11) | copy-start | bytes 2949124
  35.2 13.7 %copy-start.1 = (bf16[16,8192]{1,0:T(8,128)(2,1)S(1)}, bf16[16,8192]{1,0:T(8,128)(2,1)}, u32[]{:S(2)}) copy-start(bf16[16,8192]{1,0:T(8,128)(2,1)} %refs_0_.1) | copy-start | bytes 786436
  35.2 13.7 %copy-start.2 = (s32[16,128]{1,0:T(8,128)S(1)}, s32[16,128]{1,0:T(8,128)}, u32[]{:S(2)}) copy-start(s32[16,128]{1,0:T(8,128)} %get-tuple-element.14.pick_ref) | copy-start | bytes 24580
  35.2 13.7 %copy-start.3 = (bf16[256]{0:T(256)(128)(2,1)S(1)}, bf16[256]{0:T(256)(128)(2,1)}, u32[]{:S(2)}) copy-start(bf16[256]{0:T(256)(128)(2,1)} %refs_9_.1) | copy-start | bytes 1540
  51.4 26.3 %all-to-all-start = ((bf16[16,2,64,256]{3,2,1,0:T(8,128)(2,1)}), bf16[16,2,64,256]{3,2,1,0:T(8,128)(2,1)S(1)}, u32[]{:S(2)}, u32[]{:S(2)}) async-start(bf16[16,2,64,256]{3,2,1,0:T(8,128)(2,1)} %fresh.1), calls=%async_computation | async-start | bytes 2097152 | tf_op jit(solution)/shard_map/all_to_all | solution.py:419
